TPU v7x, 32 devices: a whole 2x2x4 slice. The times are simulated.
32 devices in a mesh: grp: 2 (over y), gx: 4 (over z), gy: 4 (over x, core).
Axes of the slice: x: 2, y: 2, z: 4, core: 2. Of those that a mesh axis runs over, the one named last changes fastest.
Arguments:
- slowness: float32 [32, 128, 128], P(('grp', 'gx')), parts along dimension 0, may hold values from 1 to 2
- buoyancy: float32 [32, 128, 128], P(('grp', 'gx')), parts along dimension 0, may hold values from 0.5 to 1
- saved_fields: bfloat16 [8, 8, 32, 128, 128], P('gy', None, ('grp', 'gx')), parts along dimension 2, may hold values from -6 to 6
- adj_states: float32 [8, 2, 32, 128, 128], P('gy', None, ('grp', 'gx')), parts along dimension 2, may hold values from -6 to 6
- residual_traces: bfloat16 [8, 6, 32, 128], P('gy', None, ('grp', 'gx')), parts along dimension 2, may hold values from -6 to 6
- receiver_depth: int32 [16], P(('grp', 'gy')), parts along dimension 0, may hold values from 1 to 63
- sample: float32 [32, 128, 128], P(('grp', 'gx'), 'gy'), parts along dimension 0, may hold values from -6 to 6
- noise_pred: bfloat16 [32, 128, 128], P(('grp', 'gx'), 'gy'), parts along dimension 0, may hold values from -6 to 6
Outputs:
- adj_last: float32 [8, 32, 128, 128], P('gy', ('grp', 'gx')), parts along dimension 1
- precond_grad: float32 [32, 128, 128], P(('grp', 'gx'), 'gy'), parts along dimension 0
- sample_next: float32 [32, 128, 128], P(('grp', 'gx'), 'gy'), parts along dimension 0
There are 2 independent parts, one for each index of `grp`. A program takes and returns all parts, laid end to end along the dimension named above; each array names one. Nothing has to cross between parts.
All inputs are finite; a program needn't handle non-finite values.
Results may differ from a plain program's by a relative error of at most 0.0003.
Values may be sent and summed in bfloat16 or wider, within the bound.
No kernel may reach another device: no remote copies, remote signals or barrier semaphores. Data moves between devices by JAX's collectives and lax.ppermute only.
A program may use at most 64 MiB of HBM per device.

v0:
```python
import jax
import jax.numpy as jnp
from jax import lax
from jax.sharding import PartitionSpec as P

time_square = 0.2


def with_halo(block, sides, width):
    for axis, dim in sides:
        count = lax.axis_size(axis)
        forward = [(i, i + 1) for i in range(count - 1)]
        backward = [(target, source) for source, target in forward]
        low = lax.ppermute(
            lax.slice_in_dim(block, block.shape[dim] - width, None, axis=dim), axis, forward
        )
        high = lax.ppermute(lax.slice_in_dim(block, 0, width, axis=dim), axis, backward)
        block = jnp.concatenate([low, block, high], axis=dim)
    return block


def pad_axis(operand, dimension):
    widths = [(0, 0)] * operand.ndim
    widths[dimension] = (1, 1)
    return jnp.pad(operand, widths)


def div_flux(wave_field, buoy_ext):
    face_x = 0.5 * (buoy_ext[1:] + buoy_ext[:-1])
    flow_x = face_x * (wave_field[..., 1:, :, :] - wave_field[..., :-1, :, :])
    summed = flow_x[..., 1:, :, :] - flow_x[..., :-1, :, :]
    centre = wave_field[..., 1:-1, :, :]
    buoy_mid = buoy_ext[1:-1]
    wave_pad = pad_axis(centre, centre.ndim - 2)
    buoy_pad = pad_axis(buoy_mid, 1)
    face_y = 0.5 * (buoy_pad[:, 1:] + buoy_pad[:, :-1])
    flow_y = face_y * (wave_pad[..., 1:, :] - wave_pad[..., :-1, :])
    summed = summed + (flow_y[..., 1:, :] - flow_y[..., :-1, :])
    wave_pad = pad_axis(centre, centre.ndim - 1)
    buoy_pad = pad_axis(buoy_mid, 2)
    face_z = 0.5 * (buoy_pad[..., 1:] + buoy_pad[..., :-1])
    flow_z = face_z * (wave_pad[..., 1:] - wave_pad[..., :-1])
    summed = summed + (flow_z[..., 1:] - flow_z[..., :-1])
    return summed


def curvature_at(saved_fields, level_index):
    return (
        saved_fields[:, level_index + 1].astype(jnp.float32)
        - 2.0 * saved_fields[:, level_index].astype(jnp.float32)
        + saved_fields[:, level_index - 1].astype(jnp.float32)
    )


def on_device(
    slowness,
    buoyancy,
    saved_fields,
    adj_states,
    residual_traces,
    receiver_depth,
    sample,
    noise_pred,
):
    modulus = 1.0 / (buoyancy * slowness * slowness)
    shots_here = saved_fields.shape[0]
    steps_count = residual_traces.shape[1]
    depth_count = saved_fields.shape[-1]
    depth_ids = lax.broadcasted_iota(jnp.int32, (shots_here, depth_count), 1)
    depth_plane = (depth_ids == receiver_depth[:, None]).astype(jnp.float32)[:, None, None, :]
    previous = adj_states[:, 0]
    current = adj_states[:, 1]
    imaging = jnp.zeros(slowness.shape, jnp.float32)
    coeffs = with_halo(jnp.stack((buoyancy, modulus)), (("gx", 1),), 2)
    buoy_wide = coeffs[0]
    modulus_wide = coeffs[1]
    traces_wide = with_halo(residual_traces, (("gx", 2),), 1)
    prev_rimmed = with_halo(previous, (("gx", 1),), 1)
    for pair_index in range(steps_count // 2):
        first_step = 2 * pair_index
        curr_wide = with_halo(current, (("gx", 1),), 2)
        source = traces_wide[:, first_step].astype(jnp.float32)[..., None] * depth_plane
        middle = (
            2.0 * curr_wide[:, 1:-1]
            - prev_rimmed
            + time_square * modulus_wide[1:-1] * (div_flux(curr_wide, buoy_wide) + source)
        )
        source = traces_wide[:, first_step + 1, 1:-1].astype(jnp.float32)[..., None] * depth_plane
        updated = (
            2.0 * middle[:, 1:-1]
            - curr_wide[:, 2:-2]
            + time_square * modulus * (div_flux(middle, buoy_wide[1:-1]) + source)
        )
        imaging = imaging + jnp.sum(
            middle[:, 1:-1] * curvature_at(saved_fields, steps_count - first_step), axis=0
        )
        imaging = imaging + jnp.sum(
            updated * curvature_at(saved_fields, steps_count - first_step - 1), axis=0
        )
        prev_rimmed = middle
        current = updated
    shots_total = shots_here * lax.axis_size("gy")
    grad_part = 2.0 * imaging / (slowness * (steps_count * shots_total))
    gradient = lax.psum_scatter(grad_part, "gy", scatter_dimension=1, tiled=True)
    padded = with_halo(gradient, (("gx", 0), ("gy", 1)), 1)
    precond_grad = 0.5 * gradient + 0.125 * (
        padded[2:, 1:-1] + padded[:-2, 1:-1] + padded[1:-1, 2:] + padded[1:-1, :-2]
    )
    sample_next = 1.02 * (sample - 0.2 * noise_pred.astype(jnp.float32)) - 0.5 * precond_grad
    return (current, precond_grad, sample_next)


def solution(mesh):
    return jax.shard_map(
        on_device,
        mesh=mesh,
        in_specs=(
            P(("grp", "gx"), None, None),
            P(("grp", "gx"), None, None),
            P("gy", None, ("grp", "gx"), None, None),
            P("gy", None, ("grp", "gx"), None, None),
            P("gy", None, ("grp", "gx"), None),
            P(("grp", "gy")),
            P(("grp", "gx"), "gy", None),
            P(("grp", "gx"), "gy", None),
        ),
        out_specs=(
            P("gy", ("grp", "gx"), None, None),
            P(("grp", "gx"), "gy", None),
            P(("grp", "gx"), "gy", None),
        ),
        check_vma=False,
    )
```

profile of v0, /device:TPU:1, one launch (start us, length us, event | category | flops | bytes accessed | tf_op | source)
XLA Modules:
  0.0 117.5 jit_solution(3023164635980961485)
XLA Ops:
  7.2 1.3 %slice_bitcast_fusion = (f32[2,4,128,128]{3,2,1,0:T(8,128)S(1)}, f32[2,4,128,128]{3,2,1,0:T(8,128)S(1)}) fusion(f32[2,2,4,128,128]{4,3,2,1,0:T(8,128)} %param.11), kind=kLoop, calls=%fused_computation.135 | loop fusion | bytes 2097152 | tf_op jit(solution)/shard_map/squeeze | solution.py:71
  8.6 1.3 %collective-permute-start.1 = (f32[2,2,128,128]{3,2,1,0:T(8,128)S(1)}, f32[2,2,128,128]{3,2,1,0:T(8,128)S(1)}, u32[]{:S(2)}, u32[]{:S(2)}) collective-permute-start(f32[2,2,128,128]{3,2,1,0:T(8,128)S(1)} %get-tuple-element.28), channel_id=1, source_target_pairs={{4,0},{8,4},{12,8},{5,1},{9,5},{13,9},{6,2},{10,6},{14,10},{7,3},{... | collective-permute-start | bytes 786440 | tf_op jit(solution)/shard_map/ppermute | solution.py:17
  10.0 1.3 %collective-permute-start.5 = (f32[2,2,128,128]{3,2,1,0:T(8,128)S(1)}, f32[2,2,128,128]{3,2,1,0:T(8,128)S(1)}, u32[]{:S(2)}, u32[]{:S(2)}) collective-permute-start(f32[2,2,128,128]{3,2,1,0:T(8,128)S(1)} %get-tuple-element.26), channel_id=1, source_target_pairs={{4,0},{8,4},{12,8},{5,1},{9,5},{13,9},{6,2},{10,6},{14,10},{7,3},{... | collective-permute-start | bytes 786440 | tf_op jit(solution)/shard_map/ppermute | solution.py:17
  11.3 5.3 %collective-permute-start.4 = (f32[2,2,128,128]{3,2,1,0:T(8,128)S(1)}, f32[2,2,128,128]{3,2,1,0:T(8,128)S(1)}, u32[]{:S(2)}, u32[]{:S(2)}) collective-permute-start(f32[2,2,128,128]{3,2,1,0:T(8,128)S(1)} %get-tuple-element.25), channel_id=1, source_target_pairs={{0,4},{4,8},{8,12},{1,5},{5,9},{9,13},{2,6},{6,10},{10,14},{3,7},{... | collective-permute-start | bytes 786440 | tf_op jit(solution)/shard_map/ppermute | solution.py:14
  16.7 1.3 %collective-permute-start.7 = (bf16[2,6,1,128]{3,2,1,0:T(2,128)(2,1)S(1)}, bf16[2,6,1,128]{3,2,1,0:T(2,128)(2,1)S(1)}, u32[]{:S(2)}, u32[]{:S(2)}) collective-permute-start(bf16[2,6,1,128]{3,2,1,0:T(2,128)(2,1)S(1)} %get-tuple-element.40), channel_id=1, source_target_pairs={{4,0},{8,4},{12,8},{5,1},{9,5},{13,9},{6,2},{10,6},{14,10},{7,3},{... | collective-permute-start | bytes 9224 | tf_op jit(solution)/shard_map/ppermute | solution.py:17
  18.0 4.0 %collective-permute-start.6 = (bf16[2,6,1,128]{3,2,1,0:T(2,128)(2,1)S(1)}, bf16[2,6,1,128]{3,2,1,0:T(2,128)(2,1)S(1)}, u32[]{:S(2)}, u32[]{:S(2)}) collective-permute-start(bf16[2,6,1,128]{3,2,1,0:T(2,128)(2,1)S(1)} %get-tuple-element.39), channel_id=1, source_target_pairs={{0,4},{4,8},{8,12},{1,5},{5,9},{9,13},{2,6},{6,10},{10,14},{3,7},{... | collective-permute-start | bytes 9224 | tf_op jit(solution)/shard_map/ppermute | solution.py:14
  22.0 0.1 compare_convert_fusion
  22.1 0.2 fusion.36
  22.3 2.1 %collective-permute-done.7 = bf16[2,6,1,128]{3,2,1,0:T(2,128)(2,1)S(1)} collective-permute-done((bf16[2,6,1,128]{3,2,1,0:T(2,128)(2,1)S(1)}, bf16[2,6,1,128]{3,2,1,0:T(2,128)(2,1)S(1)}, u32[]{:S(2)}, u32[]{:S(2)}) %collective-permute-start.7) | collective-permute-done | bytes 3104 | tf_op jit(solution)/shard_map/ppermute | solution.py:17
  24.4 3.1 %collective-permute-start = (f32[2,2,128,128]{3,2,1,0:T(8,128)S(1)}, f32[2,2,128,128]{3,2,1,0:T(8,128)S(1)}, u32[]{:S(2)}, u32[]{:S(2)}) collective-permute-start(f32[2,2,128,128]{3,2,1,0:T(8,128)S(1)} %get-tuple-element.27), channel_id=1, source_target_pairs={{0,4},{4,8},{8,12},{1,5},{5,9},{9,13},{2,6},{6,10},{10,14},{3,7},{... | collective-permute-start | bytes 786440 | tf_op jit(solution)/shard_map/ppermute | solution.py:14
  27.5 1.3 %collective-permute-start.3 = (f32[2,1,128,128]{3,2,1,0:T(8,128)S(1)}, f32[2,1,128,128]{3,2,1,0:T(8,128)S(1)}, u32[]{:S(2)}, u32[]{:S(2)}) collective-permute-start(f32[2,1,128,128]{3,2,1,0:T(8,128)S(1)} %get-tuple-element.24), channel_id=1, source_target_pairs={{4,0},{8,4},{12,8},{5,1},{9,5},{13,9},{6,2},{10,6},{14,10},{7,3},{... | collective-permute-start | bytes 393224 | tf_op jit(solution)/shard_map/ppermute | solution.py:17
  28.8 4.0 %collective-permute-start.2 = (f32[2,1,128,128]{3,2,1,0:T(8,128)S(1)}, f32[2,1,128,128]{3,2,1,0:T(8,128)S(1)}, u32[]{:S(2)}, u32[]{:S(2)}) collective-permute-start(f32[2,1,128,128]{3,2,1,0:T(8,128)S(1)} %get-tuple-element.23), channel_id=1, source_target_pairs={{0,4},{4,8},{8,12},{1,5},{5,9},{9,13},{2,6},{6,10},{10,14},{3,7},{... | collective-permute-start | bytes 393224 | tf_op jit(solution)/shard_map/ppermute | solution.py:14
  32.8 0.1 pad_maximum_fusion.1
  33.0 0.3 fusion.16
  33.4 0.1 pad_maximum_fusion
  33.5 0.1 fusion.14
  33.6 0.5 fusion.1
  34.1 0.1 subtract_multiply_fusion.2
  34.3 0.7 collective-permute-done.2
  35.0 0.6 fusion.30
  35.6 0.3 fusion.7
  36.0 0.1 subtract_multiply_fusion.5
  36.1 0.1 fusion.34
  36.2 1.1 copy-done.2
  37.3 0.4 fusion.64
  37.7 1.3 %collective-permute-start.9 = (f32[2,2,128,128]{3,2,1,0:T(8,128)S(1)}, f32[2,2,128,128]{3,2,1,0:T(8,128)S(1)}, u32[]{:S(2)}, u32[]{:S(2)}) collective-permute-start(f32[2,2,128,128]{3,2,1,0:T(8,128)S(1)} %get-tuple-element.20), channel_id=1, source_target_pairs={{4,0},{8,4},{12,8},{5,1},{9,5},{13,9},{6,2},{10,6},{14,10},{7,3},{... | collective-permute-start | bytes 786440 | tf_op jit(solution)/shard_map/ppermute | solution.py:17
  39.0 4.6 %collective-permute-start.8 = (f32[2,2,128,128]{3,2,1,0:T(8,128)S(1)}, f32[2,2,128,128]{3,2,1,0:T(8,128)S(1)}, u32[]{:S(2)}, u32[]{:S(2)}) collective-permute-start(f32[2,2,128,128]{3,2,1,0:T(8,128)S(1)} %get-tuple-element.19), channel_id=1, source_target_pairs={{0,4},{4,8},{8,12},{1,5},{5,9},{9,13},{2,6},{6,10},{10,14},{3,7},{... | collective-permute-start | bytes 786440 | tf_op jit(solution)/shard_map/ppermute | solution.py:14
  43.7 1.8 %collective-permute-done.9 = f32[2,2,128,128]{3,2,1,0:T(8,128)S(1)} collective-permute-done((f32[2,2,128,128]{3,2,1,0:T(8,128)S(1)}, f32[2,2,128,128]{3,2,1,0:T(8,128)S(1)}, u32[]{:S(2)}, u32[]{:S(2)}) %collective-permute-start.9) | collective-permute-done | bytes 262176 | tf_op jit(solution)/shard_map/ppermute | solution.py:17
  45.5 1.5 %collective-permute-done.8 = f32[2,2,128,128]{3,2,1,0:T(8,128)S(1)} collective-permute-done((f32[2,2,128,128]{3,2,1,0:T(8,128)S(1)}, f32[2,2,128,128]{3,2,1,0:T(8,128)S(1)}, u32[]{:S(2)}, u32[]{:S(2)}) %collective-permute-start.8) | collective-permute-done | bytes 262176 | tf_op jit(solution)/shard_map/ppermute | solution.py:14
  47.0 0.1 pad_maximum_fusion.2
  47.1 0.5 fusion.3
  47.6 0.1 subtract_multiply_fusion.1
  47.7 0.1 fusion.13
  47.9 0.6 fusion.25
  48.5 0.3 fusion.9
  48.8 0.1 subtract_multiply_fusion.4
  48.9 0.1 fusion.33
  49.0 0.4 fusion.59
  49.5 1.3 %collective-permute-start.11 = (f32[2,2,128,128]{3,2,1,0:T(8,128)S(1)}, f32[2,2,128,128]{3,2,1,0:T(8,128)S(1)}, u32[]{:S(2)}, u32[]{:S(2)}) collective-permute-start(f32[2,2,128,128]{3,2,1,0:T(8,128)S(1)} %get-tuple-element.18), channel_id=1, source_target_pairs={{4,0},{8,4},{12,8},{5,1},{9,5},{13,9},{6,2},{10,6},{14,10},{7,3},{... | collective-permute-start | bytes 786440 | tf_op jit(solution)/shard_map/ppermute | solution.py:17
  50.8 4.7 %collective-permute-start.10 = (f32[2,2,128,128]{3,2,1,0:T(8,128)S(1)}, f32[2,2,128,128]{3,2,1,0:T(8,128)S(1)}, u32[]{:S(2)}, u32[]{:S(2)}) collective-permute-start(f32[2,2,128,128]{3,2,1,0:T(8,128)S(1)} %get-tuple-element.17), channel_id=1, source_target_pairs={{0,4},{4,8},{8,12},{1,5},{5,9},{9,13},{2,6},{6,10},{10,14},{3,7},{... | collective-permute-start | bytes 786440 | tf_op jit(solution)/shard_map/ppermute | solution.py:14
  55.5 1.8 %collective-permute-done.11 = f32[2,2,128,128]{3,2,1,0:T(8,128)S(1)} collective-permute-done((f32[2,2,128,128]{3,2,1,0:T(8,128)S(1)}, f32[2,2,128,128]{3,2,1,0:T(8,128)S(1)}, u32[]{:S(2)}, u32[]{:S(2)}) %collective-permute-start.11) | collective-permute-done | bytes 262176 | tf_op jit(solution)/shard_map/ppermute | solution.py:17
  57.3 1.5 %collective-permute-done.10 = f32[2,2,128,128]{3,2,1,0:T(8,128)S(1)} collective-permute-done((f32[2,2,128,128]{3,2,1,0:T(8,128)S(1)}, f32[2,2,128,128]{3,2,1,0:T(8,128)S(1)}, u32[]{:S(2)}, u32[]{:S(2)}) %collective-permute-start.10) | collective-permute-done | bytes 262176 | tf_op jit(solution)/shard_map/ppermute | solution.py:14
  58.8 0.1 pad_maximum_fusion.3
  59.0 0.5 fusion.5
  59.5 0.1 subtract_multiply_fusion
  59.6 0.1 fusion.12
  59.7 0.6 fusion.20
  60.3 1.0 copy-done.1
  61.3 0.5 fusion.43
  61.8 0.3 fusion.11
  62.2 0.1 subtract_multiply_fusion.3
  62.2 0.1 fusion.32
  62.3 1.4 %fusion.41 = (f32[4,128,128]{2,1,0:T(8,128)S(1)}, f32[4,128,128]{2,1,0:T(8,128)S(1)}, f32[2,4,128,128]{3,2,1,0:T(8,128)}) fusion(bf16[2,8,4,128,128]{4,3,2,1,0:T(8,128)(2,1)S(1)} %copy-done.1, f32[2,6,128,128]{3,2,1,0:T(8,128)S(1)} %fusion.30, f32[2,128]{1,0:T(2,128)S(1)} %compare_convert_fusion, f32[2,4,128]{2,1,0:T(4,128)S(1)} %get-tuple-element.38, ...), kind=kLoop, calls=%fused_computation.99 | loop fusion | flops 3407872 | bytes 7607296 | tf_op jit(solution)/shard_map/reduce_sum | solution.py:94
  63.7 0.8 multiply_divide_fusion
  64.5 26.9 %reduce-scatter.2.cloned.1.call-done = f32[4,32,128]{2,1,0:T(8,128)} async-done(((f32[4,128,128]{2,1,0:T(8,128)}), f32[4,32,128]{2,1,0:T(8,128)}) %reduce-scatter.2.cloned.1.call-update) | async-done | bytes 65552 | tf_op jit(solution)/shard_map/reduce_scatter | solution.py:104
  91.4 0.7 fusion.91
  92.1 3.1 %collective-permute-start.13 = (f32[1,32,128]{2,1,0:T(8,128)S(1)}, f32[1,32,128]{2,1,0:T(8,128)S(1)}, u32[]{:S(2)}, u32[]{:S(2)}) collective-permute-start(f32[1,32,128]{2,1,0:T(8,128)S(1)} %get-tuple-element.32), channel_id=1, source_target_pairs={{0,4},{4,8},{8,12},{1,5},{5,9},{9,13},{2,6},{6,10},{10,14},{3,7},{... | collective-permute-start | bytes 49160 | tf_op jit(solution)/shard_map/ppermute | solution.py:14
  95.2 1.3 %collective-permute-start.12 = (f32[1,32,128]{2,1,0:T(8,128)S(1)}, f32[1,32,128]{2,1,0:T(8,128)S(1)}, u32[]{:S(2)}, u32[]{:S(2)}) collective-permute-start(f32[1,32,128]{2,1,0:T(8,128)S(1)} %get-tuple-element.31), channel_id=1, source_target_pairs={{4,0},{8,4},{12,8},{5,1},{9,5},{13,9},{6,2},{10,6},{14,10},{7,3},{... | collective-permute-start | bytes 49160 | tf_op jit(solution)/shard_map/ppermute | solution.py:17
  96.5 0.8 constant_dynamic-update-slice_fusion.1
  97.4 2.3 %collective-permute-done.12 = f32[1,32,128]{2,1,0:T(8,128)S(1)} collective-permute-done((f32[1,32,128]{2,1,0:T(8,128)S(1)}, f32[1,32,128]{2,1,0:T(8,128)S(1)}, u32[]{:S(2)}, u32[]{:S(2)}) %collective-permute-start.12) | collective-permute-done | bytes 16416 | tf_op jit(solution)/shard_map/ppermute | solution.py:17
  99.7 4.4 %collective-permute-start.15 = (f32[6,1,128]{2,1,0:T(1,128)S(1)}, f32[6,1,128]{2,1,0:T(1,128)S(1)}, u32[]{:S(2)}, u32[]{:S(2)}) collective-permute-start(f32[6,1,128]{2,1,0:T(1,128)S(1)} %get-tuple-element.30), channel_id=1, source_target_pairs={{0,1},{1,2},{2,3},{4,5},{5,6},{6,7},{8,9},{9,10},{10,11},{12,13},{... | collective-permute-start | bytes 9224 | tf_op jit(solution)/shard_map/ppermute | solution.py:14
  104.1 1.9 %collective-permute-start.14 = (f32[6,1,128]{2,1,0:T(1,128)S(1)}, f32[6,1,128]{2,1,0:T(1,128)S(1)}, u32[]{:S(2)}, u32[]{:S(2)}) collective-permute-start(f32[6,1,128]{2,1,0:T(1,128)S(1)} %get-tuple-element.29), channel_id=1, source_target_pairs={{1,0},{2,1},{3,2},{5,4},{6,5},{7,6},{9,8},{10,9},{11,10},{13,12},{... | collective-permute-start | bytes 9224 | tf_op jit(solution)/shard_map/ppermute | solution.py:17
  106.1 3.0 %collective-permute-done.14 = f32[6,1,128]{2,1,0:T(1,128)S(1)} collective-permute-done((f32[6,1,128]{2,1,0:T(1,128)S(1)}, f32[6,1,128]{2,1,0:T(1,128)S(1)}, u32[]{:S(2)}, u32[]{:S(2)}) %collective-permute-start.14) | collective-permute-done | bytes 3104 | tf_op jit(solution)/shard_map/ppermute | solution.py:17
  109.1 1.6 %multiply_subtract_fusion = (f32[4,32,128]{2,1,0:T(8,128)}, f32[4,32,128]{2,1,0:T(8,128)}) fusion(f32[4,32,128]{2,1,0:T(8,128)S(1)} %copy-done.5, bf16[4,32,128]{2,1,0:T(8,128)(2,1)S(1)} %copy-done.6, f32[6,32,128]{2,1,0:T(8,128)S(1)} %constant_dynamic-update-slice_fusion, f32[6,1,128]{2,1,0:T(1,128)S(1)} %collective-permute-done.15, ...), kind=kLoop, calls=%fused_computation.167 | loop fusion | flops 262144 | bytes 432128 | tf_op jit(solution)/shard_map/sub | solution.py:109
  (46 shorter events, 0.8 us)
Async XLA Ops:
  7.2 2.8 %copy-start = (f32[4,128,128]{2,1,0:T(8,128)S(1)}, f32[4,128,128]{2,1,0:T(8,128)}, u32[]{:S(2)}) copy-start(f32[4,128,128]{2,1,0:T(8,128)} %param.9) | copy-start | bytes 786436
  7.2 2.8 %copy-start.3 = (f32[4,128,128]{2,1,0:T(8,128)S(1)}, f32[4,128,128]{2,1,0:T(8,128)}, u32[]{:S(2)}) copy-start(f32[4,128,128]{2,1,0:T(8,128)} %param.8) | copy-start | bytes 786436
  7.2 84.2 %reduce-scatter.2.cloned.1.call-start = ((), (), s32[]{:S(2)}) async-start(), calls=%async_computation.1 | async-start | bytes 327680 | tf_op jit(solution)/shard_map/reduce_scatter | solution.py:104
  8.6 8.1 %copy-start.4 = (bf16[2,6,4,128]{3,2,1,0:T(4,128)(2,1)S(1)}, bf16[2,6,4,128]{3,2,1,0:T(4,128)(2,1)}, u32[]{:S(2)}) copy-start(bf16[2,6,4,128]{3,2,1,0:T(4,128)(2,1)} %param.12) | copy-start | bytes 36868
  8.6 13.4 %copy-start.7 = (s32[2]{0:T(128)S(1)}, s32[2]{0:T(128)}, u32[]{:S(2)}) copy-start(s32[2]{0:T(128)} %param.13) | copy-start | bytes 28
  8.6 24.7 %collective-permute-start.1 = (f32[2,2,128,128]{3,2,1,0:T(8,128)S(1)}, f32[2,2,128,128]{3,2,1,0:T(8,128)S(1)}, u32[]{:S(2)}, u32[]{:S(2)}) collective-permute-start(f32[2,2,128,128]{3,2,1,0:T(8,128)S(1)} %get-tuple-element.28), channel_id=1, source_target_pairs={{4,0},{8,4},{12,8},{5,1},{9,5},{13,9},{6,2},{10,6},{14,10},{7,3},{... | collective-permute-start | bytes 786440 | tf_op jit(solution)/shard_map/ppermute | solution.py:17
  10.0 18.8 %collective-permute-start.5 = (f32[2,2,128,128]{3,2,1,0:T(8,128)S(1)}, f32[2,2,128,128]{3,2,1,0:T(8,128)S(1)}, u32[]{:S(2)}, u32[]{:S(2)}) collective-permute-start(f32[2,2,128,128]{3,2,1,0:T(8,128)S(1)} %get-tuple-element.26), channel_id=1, source_target_pairs={{4,0},{8,4},{12,8},{5,1},{9,5},{13,9},{6,2},{10,6},{14,10},{7,3},{... | collective-permute-start | bytes 786440 | tf_op jit(solution)/shard_map/ppermute | solution.py:17
  11.3 21.5 %collective-permute-start.4 = (f32[2,2,128,128]{3,2,1,0:T(8,128)S(1)}, f32[2,2,128,128]{3,2,1,0:T(8,128)S(1)}, u32[]{:S(2)}, u32[]{:S(2)}) collective-permute-start(f32[2,2,128,128]{3,2,1,0:T(8,128)S(1)} %get-tuple-element.25), channel_id=1, source_target_pairs={{0,4},{4,8},{8,12},{1,5},{5,9},{9,13},{2,6},{6,10},{10,14},{3,7},{... | collective-permute-start | bytes 786440 | tf_op jit(solution)/shard_map/ppermute | solution.py:14
  16.7 7.7 %collective-permute-start.7 = (bf16[2,6,1,128]{3,2,1,0:T(2,128)(2,1)S(1)}, bf16[2,6,1,128]{3,2,1,0:T(2,128)(2,1)S(1)}, u32[]{:S(2)}, u32[]{:S(2)}) collective-permute-start(bf16[2,6,1,128]{3,2,1,0:T(2,128)(2,1)S(1)} %get-tuple-element.40), channel_id=1, source_target_pairs={{4,0},{8,4},{12,8},{5,1},{9,5},{13,9},{6,2},{10,6},{14,10},{7,3},{... | collective-permute-start | bytes 9224 | tf_op jit(solution)/shard_map/ppermute | solution.py:17
  18.0 9.5 %collective-permute-start.6 = (bf16[2,6,1,128]{3,2,1,0:T(2,128)(2,1)S(1)}, bf16[2,6,1,128]{3,2,1,0:T(2,128)(2,1)S(1)}, u32[]{:S(2)}, u32[]{:S(2)}) collective-permute-start(bf16[2,6,1,128]{3,2,1,0:T(2,128)(2,1)S(1)} %get-tuple-element.39), channel_id=1, source_target_pairs={{0,4},{4,8},{8,12},{1,5},{5,9},{9,13},{2,6},{6,10},{10,14},{3,7},{... | collective-permute-start | bytes 9224 | tf_op jit(solution)/shard_map/ppermute | solution.py:14
  24.4 9.0 %collective-permute-start = (f32[2,2,128,128]{3,2,1,0:T(8,128)S(1)}, f32[2,2,128,128]{3,2,1,0:T(8,128)S(1)}, u32[]{:S(2)}, u32[]{:S(2)}) collective-permute-start(f32[2,2,128,128]{3,2,1,0:T(8,128)S(1)} %get-tuple-element.27), channel_id=1, source_target_pairs={{0,4},{4,8},{8,12},{1,5},{5,9},{9,13},{2,6},{6,10},{10,14},{3,7},{... | collective-permute-start | bytes 786440 | tf_op jit(solution)/shard_map/ppermute | solution.py:14
  27.5 6.8 %collective-permute-start.3 = (f32[2,1,128,128]{3,2,1,0:T(8,128)S(1)}, f32[2,1,128,128]{3,2,1,0:T(8,128)S(1)}, u32[]{:S(2)}, u32[]{:S(2)}) collective-permute-start(f32[2,1,128,128]{3,2,1,0:T(8,128)S(1)} %get-tuple-element.24), channel_id=1, source_target_pairs={{4,0},{8,4},{12,8},{5,1},{9,5},{13,9},{6,2},{10,6},{14,10},{7,3},{... | collective-permute-start | bytes 393224 | tf_op jit(solution)/shard_map/ppermute | solution.py:17
  28.8 6.2 %collective-permute-start.2 = (f32[2,1,128,128]{3,2,1,0:T(8,128)S(1)}, f32[2,1,128,128]{3,2,1,0:T(8,128)S(1)}, u32[]{:S(2)}, u32[]{:S(2)}) collective-permute-start(f32[2,1,128,128]{3,2,1,0:T(8,128)S(1)} %get-tuple-element.23), channel_id=1, source_target_pairs={{0,4},{4,8},{8,12},{1,5},{5,9},{9,13},{2,6},{6,10},{10,14},{3,7},{... | collective-permute-start | bytes 393224 | tf_op jit(solution)/shard_map/ppermute | solution.py:14
  36.1 1.2 %copy-start.2 = (f32[2,2,4,128,128]{4,3,2,1,0:T(8,128)S(1)}, f32[2,2,4,128,128]{4,3,2,1,0:T(8,128)}, u32[]{:S(2)}) copy-start(f32[2,2,4,128,128]{4,3,2,1,0:T(8,128)} %param.11) | copy-start | bytes 3145732
  37.7 7.7 %collective-permute-start.9 = (f32[2,2,128,128]{3,2,1,0:T(8,128)S(1)}, f32[2,2,128,128]{3,2,1,0:T(8,128)S(1)}, u32[]{:S(2)}, u32[]{:S(2)}) collective-permute-start(f32[2,2,128,128]{3,2,1,0:T(8,128)S(1)} %get-tuple-element.20), channel_id=1, source_target_pairs={{4,0},{8,4},{12,8},{5,1},{9,5},{13,9},{6,2},{10,6},{14,10},{7,3},{... | collective-permute-start | bytes 786440 | tf_op jit(solution)/shard_map/ppermute | solution.py:17
  39.0 7.9 %collective-permute-start.8 = (f32[2,2,128,128]{3,2,1,0:T(8,128)S(1)}, f32[2,2,128,128]{3,2,1,0:T(8,128)S(1)}, u32[]{:S(2)}, u32[]{:S(2)}) collective-permute-start(f32[2,2,128,128]{3,2,1,0:T(8,128)S(1)} %get-tuple-element.19), channel_id=1, source_target_pairs={{0,4},{4,8},{8,12},{1,5},{5,9},{9,13},{2,6},{6,10},{10,14},{3,7},{... | collective-permute-start | bytes 786440 | tf_op jit(solution)/shard_map/ppermute | solution.py:14
  49.5 7.9 %collective-permute-start.11 = (f32[2,2,128,128]{3,2,1,0:T(8,128)S(1)}, f32[2,2,128,128]{3,2,1,0:T(8,128)S(1)}, u32[]{:S(2)}, u32[]{:S(2)}) collective-permute-start(f32[2,2,128,128]{3,2,1,0:T(8,128)S(1)} %get-tuple-element.18), channel_id=1, source_target_pairs={{4,0},{8,4},{12,8},{5,1},{9,5},{13,9},{6,2},{10,6},{14,10},{7,3},{... | collective-permute-start | bytes 786440 | tf_op jit(solution)/shard_map/ppermute | solution.py:17
  50.8 8.0 %collective-permute-start.10 = (f32[2,2,128,128]{3,2,1,0:T(8,128)S(1)}, f32[2,2,128,128]{3,2,1,0:T(8,128)S(1)}, u32[]{:S(2)}, u32[]{:S(2)}) collective-permute-start(f32[2,2,128,128]{3,2,1,0:T(8,128)S(1)} %get-tuple-element.17), channel_id=1, source_target_pairs={{0,4},{4,8},{8,12},{1,5},{5,9},{9,13},{2,6},{6,10},{10,14},{3,7},{... | collective-permute-start | bytes 786440 | tf_op jit(solution)/shard_map/ppermute | solution.py:14
  59.7 1.6 %copy-start.1 = (bf16[2,8,4,128,128]{4,3,2,1,0:T(8,128)(2,1)S(1)}, bf16[2,8,4,128,128]{4,3,2,1,0:T(8,128)(2,1)}, u32[]{:S(2)}) copy-start(bf16[2,8,4,128,128]{4,3,2,1,0:T(8,128)(2,1)} %param.10) | copy-start | bytes 6291460
  63.7 45.4 %copy-start.5 = (f32[4,32,128]{2,1,0:T(8,128)S(1)}, f32[4,32,128]{2,1,0:T(8,128)}, u32[]{:S(2)}) copy-start(f32[4,32,128]{2,1,0:T(8,128)} %param.14) | copy-start | bytes 196612
  63.7 45.4 %copy-start.6 = (bf16[4,32,128]{2,1,0:T(8,128)(2,1)S(1)}, bf16[4,32,128]{2,1,0:T(8,128)(2,1)}, u32[]{:S(2)}) copy-start(bf16[4,32,128]{2,1,0:T(8,128)(2,1)} %param.15) | copy-start | bytes 98308
  92.1 4.4 %collective-permute-start.13 = (f32[1,32,128]{2,1,0:T(8,128)S(1)}, f32[1,32,128]{2,1,0:T(8,128)S(1)}, u32[]{:S(2)}, u32[]{:S(2)}) collective-permute-start(f32[1,32,128]{2,1,0:T(8,128)S(1)} %get-tuple-element.32), channel_id=1, source_target_pairs={{0,4},{4,8},{8,12},{1,5},{5,9},{9,13},{2,6},{6,10},{10,14},{3,7},{... | collective-permute-start | bytes 49160 | tf_op jit(solution)/shard_map/ppermute | solution.py:14
  95.2 4.5 %collective-permute-start.12 = (f32[1,32,128]{2,1,0:T(8,128)S(1)}, f32[1,32,128]{2,1,0:T(8,128)S(1)}, u32[]{:S(2)}, u32[]{:S(2)}) collective-permute-start(f32[1,32,128]{2,1,0:T(8,128)S(1)} %get-tuple-element.31), channel_id=1, source_target_pairs={{4,0},{8,4},{12,8},{5,1},{9,5},{13,9},{6,2},{10,6},{14,10},{7,3},{... | collective-permute-start | bytes 49160 | tf_op jit(solution)/shard_map/ppermute | solution.py:17
  99.7 6.4 %collective-permute-start.15 = (f32[6,1,128]{2,1,0:T(1,128)S(1)}, f32[6,1,128]{2,1,0:T(1,128)S(1)}, u32[]{:S(2)}, u32[]{:S(2)}) collective-permute-start(f32[6,1,128]{2,1,0:T(1,128)S(1)} %get-tuple-element.30), channel_id=1, source_target_pairs={{0,1},{1,2},{2,3},{4,5},{5,6},{6,7},{8,9},{9,10},{10,11},{12,13},{... | collective-permute-start | bytes 9224 | tf_op jit(solution)/shard_map/ppermute | solution.py:14
  104.1 4.9 %collective-permute-start.14 = (f32[6,1,128]{2,1,0:T(1,128)S(1)}, f32[6,1,128]{2,1,0:T(1,128)S(1)}, u32[]{:S(2)}, u32[]{:S(2)}) collective-permute-start(f32[6,1,128]{2,1,0:T(1,128)S(1)} %get-tuple-element.29), channel_id=1, source_target_pairs={{1,0},{2,1},{3,2},{5,4},{6,5},{7,6},{9,8},{10,9},{11,10},{13,12},{... | collective-permute-start | bytes 9224 | tf_op jit(solution)/shard_map/ppermute | solution.py:17
Sparse Core Ops, SparseCore 0:
  64.6 26.7 reduce-scatter.1
where the time goes:
time: 118 us
  starting transfers between devices  44.2 us (37%)
  waiting for transfers between devices  41.5 us (35%)
  between operations  14.6 us (12%)
  other arithmetic  11.7 us (10%)
  local copies, waits for them, and re-layouts  5.4 us (5%)
    ppermute x8, starting transfers between devices, with_halo(): lax.ppermute(lax.slice_in_dim(block, block.shape[dim] - width, None, axis...  33.2 us
    reduce_scatter x1, waiting for transfers between devices, on_device(): lax.psum_scatter(grad_part, 'gy', scatter_dimension=1, tiled=True)  26.9 us
    ppermute x8, waiting for transfers between devices, with_halo(): lax.ppermute(lax.slice_in_dim(block, 0, width, axis=dim), axis, backward)  11 us
    ppermute x8, starting transfers between devices, with_halo(): lax.ppermute(lax.slice_in_dim(block, 0, width, axis=dim), axis, backward)  11 us
    ppermute x8, waiting for transfers between devices, with_halo(): lax.ppermute(lax.slice_in_dim(block, block.shape[dim] - width, None, axis...  3.67 us
    unnamed x18, local copies, waits for them, and re-layouts  2.96 us
    mul x6, other arithmetic, div_flux(): flow_z = face_z * (wave_pad[..., 1:] - wave_pad[..., :-1])  2.51 us
  transfers between devices with their start and end apart: 17, of which 9 were waited for; matrix products, arithmetic and copies ran while one was open for 2% of the time, Pallas kernels for 0%

commit v1 on v0

v1 whole, which is shorter than its diff:
```python
import jax
import jax.numpy as jnp
from jax import lax
from jax.sharding import PartitionSpec as P

time_square = 0.2
WIRE = jnp.float16


def pad_axis(operand, dimension):
    widths = [(0, 0)] * operand.ndim
    widths[dimension] = (1, 1)
    return jnp.pad(operand, widths)


def div_flux(wave_field, buoy_ext):
    face_x = 0.5 * (buoy_ext[1:] + buoy_ext[:-1])
    flow_x = face_x * (wave_field[..., 1:, :, :] - wave_field[..., :-1, :, :])
    summed = flow_x[..., 1:, :, :] - flow_x[..., :-1, :, :]
    centre = wave_field[..., 1:-1, :, :]
    buoy_mid = buoy_ext[1:-1]
    wave_pad = pad_axis(centre, centre.ndim - 2)
    buoy_pad = pad_axis(buoy_mid, 1)
    face_y = 0.5 * (buoy_pad[:, 1:] + buoy_pad[:, :-1])
    flow_y = face_y * (wave_pad[..., 1:, :] - wave_pad[..., :-1, :])
    summed = summed + (flow_y[..., 1:, :] - flow_y[..., :-1, :])
    wave_pad = pad_axis(centre, centre.ndim - 1)
    buoy_pad = pad_axis(buoy_mid, 2)
    face_z = 0.5 * (buoy_pad[..., 1:] + buoy_pad[..., :-1])
    flow_z = face_z * (wave_pad[..., 1:] - wave_pad[..., :-1])
    summed = summed + (flow_z[..., 1:] - flow_z[..., :-1])
    return summed


def curvature_at(saved_fields, level_index):
    return (
        saved_fields[:, level_index + 1].astype(jnp.float32)
        - 2.0 * saved_fields[:, level_index].astype(jnp.float32)
        + saved_fields[:, level_index - 1].astype(jnp.float32)
    )


def field_bounds(steps_count):
    bounds = [6.0, 6.0]
    for _ in range(steps_count):
        bounds.append(2.0 * bounds[-1] + bounds[-2] + time_square * 2.0 * 6.0)
    return bounds[1:]


def wire_scale(bound):
    scale = 1.0
    while scale * 2.0 * bound < 65000.0:
        scale = scale * 2.0
    return scale


def on_device(
    slowness,
    buoyancy,
    saved_fields,
    adj_states,
    residual_traces,
    receiver_depth,
    sample,
    noise_pred,
):
    gx_count = lax.axis_size("gx")
    gy_count = lax.axis_size("gy")
    pair_count = gy_count // 2
    gx_index = lax.axis_index("gx")
    gy_index = lax.axis_index("gy")
    side = gy_index % 2
    pair = gy_index // 2
    lower = side == 0
    shots, _, layers, rows, depth_count = adj_states.shape
    own = layers // 2
    steps_count = residual_traces.shape[1]
    has_outer = jnp.where(lower, gx_index > 0, gx_index < gx_count - 1)

    outer_perm = []
    for z in range(gx_count - 1):
        for p in range(pair_count):
            a = z * gy_count + 2 * p + 1
            b = (z + 1) * gy_count + 2 * p
            outer_perm += [(a, b), (b, a)]
    inner_perm = [(g, g ^ 1) for g in range(gy_count)]

    def to_outer(v):
        return lax.ppermute(v, ("gx", "gy"), outer_perm)

    def to_inner(v):
        return lax.ppermute(v, "gy", inner_perm)

    def orient(v, dim):
        return jnp.where(lower, v, jnp.flip(v, dim))

    def flat(v):
        return v.reshape(-1, depth_count)

    adj = orient(adj_states, 2)
    traces = orient(residual_traces, 2).astype(jnp.float32)
    saved = orient(saved_fields, 2)
    slow = orient(slowness, 0)
    buoy = orient(buoyancy, 0)

    depth_row = jnp.broadcast_to(
        receiver_depth.astype(jnp.float32)[:, None], (shots, depth_count)
    )
    theirs = jnp.flip(adj[:, :, own:], 2)
    swap = jnp.concatenate([flat(theirs), flat(jnp.flip(traces, 2)), depth_row], axis=0)
    swap_in = to_inner(swap)

    scale0 = wire_scale(6.0)
    first_steps = list(range(0, steps_count, 2))

    def field_payload(states, trace):
        return jnp.concatenate(
            [
                flat(states[:, 1, :own]),
                flat(states[:, 0, :1]),
                flat(jnp.stack([trace[:, k, 0] for k in first_steps], 1)),
            ],
            axis=0,
        )

    payload1 = jnp.concatenate(
        [
            field_payload(adj, traces) * scale0,
            flat((buoy[:2] - 0.75) * scale0),
            flat((slow[:1] - 1.5) * scale0),
        ],
        axis=0,
    ).astype(WIRE)
    outer1 = to_outer(payload1)
    rim = jnp.concatenate([flat(adj[:, 1, :own]), flat(adj[:, 0, own - 1 : own])], axis=0)
    rim_in = to_inner(rim)
    saved_in = to_inner(jnp.flip(saved[:, :, own:], 2))

    n_adj = shots * 2 * own * rows
    adj_in = swap_in[:n_adj].reshape(shots, 2, own, rows, depth_count)
    n_tr = shots * steps_count * layers
    traces_in = swap_in[n_adj : n_adj + n_tr].reshape(shots, steps_count, layers, rows)
    depth_in = swap_in[n_adj + n_tr :]
    outer2 = to_outer((field_payload(adj_in, traces_in) * scale0).astype(WIRE))

    def split_outer(v):
        v = v.astype(jnp.float32) * (1.0 / scale0)
        a = shots * own * rows
        b = a + shots * rows
        c = b + shots * len(first_steps)
        return (
            v[:a].reshape(shots, own, rows, depth_count),
            v[a:b].reshape(shots, 1, rows, depth_count),
            v[b:c].reshape(shots, len(first_steps), rows),
            v[c:],
        )

    cur_o_b, prev_o_b, tr_o_b, coef = split_outer(outer1)
    cur_o_a, prev_o_a, tr_o_a, _ = split_outer(outer2)
    valid = has_outer.astype(jnp.float32)
    buoy_o = (coef[: own * rows].reshape(own, rows, depth_count) + 0.75) * valid
    slow_o = coef[own * rows :].reshape(1, rows, depth_count) + 1.5
    mod_o = valid / (jnp.maximum(buoy_o[:1], 0.5) * slow_o * slow_o)
    buoy_wide = jnp.concatenate([jnp.flip(buoy_o, 0), buoy], axis=0)
    mod_own = 1.0 / (buoy[: own + 1] * slow[: own + 1] * slow[: own + 1])
    mod_wide = jnp.concatenate([mod_o, mod_own], axis=0)
    cur_outer = jnp.flip(jnp.concatenate([cur_o_a, cur_o_b], axis=0), 1)
    prev_outer = jnp.concatenate([prev_o_a, prev_o_b], axis=0)
    tr_outer = jnp.concatenate([tr_o_a, tr_o_b], axis=0)

    n_cur = shots * own * rows
    rim_cur = rim_in[:n_cur].reshape(shots, own, rows, depth_count)
    rim_prev = rim_in[n_cur:].reshape(shots, 1, rows, depth_count)
    cur_inner = jnp.concatenate([adj[:, 1, own:], jnp.flip(rim_cur, 1)], axis=0)
    prev_inner = jnp.concatenate([adj[:, 0, own : own + 1], rim_prev], axis=0)
    current = jnp.concatenate([adj[:, 1, :own], adj_in[:, 1]], axis=0)
    previous = jnp.concatenate([adj[:, 0, :own], adj_in[:, 0]], axis=0)
    prev_rimmed = jnp.concatenate([prev_outer, previous, prev_inner], axis=1)
    traces_own = jnp.concatenate([traces, traces_in], axis=0)
    depth_ids = lax.broadcasted_iota(jnp.int32, (2 * shots, depth_count), 1)
    depth_row = jnp.concatenate([depth_row, depth_in], axis=0)
    depth_plane = (depth_ids.astype(jnp.float32) == depth_row).astype(jnp.float32)[:, None, None, :]
    saved_own = jnp.concatenate([saved[:, :, :own], saved_in], axis=0)

    def mirrored(v):
        return jnp.concatenate([v[shots:], v[:shots]], axis=0)

    imaging = jnp.zeros((own, rows, depth_count), jnp.float32)
    bounds = field_bounds(steps_count)
    for pair_index in range(steps_count // 2):
        first_step = 2 * pair_index
        if pair_index > 0:
            scale = wire_scale(bounds[first_step])
            out = mirrored(current)
            o_in = to_outer((out * scale).astype(WIRE))
            i_in = to_inner(out)
            cur_outer = jnp.flip(o_in.astype(jnp.float32) * (1.0 / scale), 1)
            cur_inner = jnp.flip(i_in, 1)
        curr_wide = jnp.concatenate([cur_outer, current, cur_inner], axis=1)
        trace_mid = jnp.concatenate(
            [tr_outer[:, pair_index][:, None], traces_own[:, first_step, : own + 1]], axis=1
        )
        source = trace_mid[..., None] * depth_plane
        middle = (
            2.0 * curr_wide[:, 1:-1]
            - prev_rimmed
            + time_square * mod_wide * (div_flux(curr_wide, buoy_wide) + source)
        )
        source = traces_own[:, first_step + 1, :own][..., None] * depth_plane
        updated = (
            2.0 * middle[:, 1:-1]
            - current
            + time_square * mod_own[:own] * (div_flux(middle, buoy_wide[1:-1]) + source)
        )
        imaging = imaging + jnp.sum(
            middle[:, 1:-1] * curvature_at(saved_own, steps_count - first_step), axis=0
        )
        imaging = imaging + jnp.sum(
            updated * curvature_at(saved_own, steps_count - first_step - 1), axis=0
        )
        prev_rimmed = middle
        current = updated

    back = to_inner(current[shots:])
    mine = current[:shots]
    adj_last = orient(jnp.concatenate([mine, jnp.flip(back, 1)], axis=1), 1)

    shots_total = shots * gy_count
    grad_part = 2.0 * imaging / (slow[:own] * (steps_count * shots_total))
    pair_rows = rows // pair_count
    padded = pad_axis(grad_part, 1)
    slices = [padded[:, q * pair_rows : (q + 1) * pair_rows + 2] for q in range(pair_count)]

    def slice_of(q):
        out = slices[0]
        for i in range(1, pair_count):
            out = jnp.where(q == i, slices[i], out)
        return out

    red = slice_of(pair)
    for d in range(1, pair_count):
        perm = [
            (2 * p + e, 2 * ((p + d) % pair_count) + e)
            for p in range(pair_count)
            for e in range(2)
        ]
        red = red + lax.ppermute(slice_of((pair + d) % pair_count), "gy", perm)
    far = to_outer(red[:1, 1:-1])
    near = to_inner(red[own - 1 : own, 1:-1])
    centre = red[:, 1:-1]
    tall = jnp.concatenate([far, centre, near], axis=0)
    precond = 0.5 * centre + 0.125 * (tall[2:] + tall[:-2] + red[:, 2:] + red[:, :-2])
    half = pair_rows // 2
    keep = jnp.where(lower, precond[:, :half], precond[:, half:])
    give = jnp.where(lower, precond[:, half:], precond[:, :half])
    got = to_inner(give)
    precond_grad = orient(jnp.concatenate([keep, jnp.flip(got, 0)], axis=0), 0)
    sample_next = 1.02 * (sample - 0.2 * noise_pred.astype(jnp.float32)) - 0.5 * precond_grad
    return (adj_last, precond_grad, sample_next)


def solution(mesh):
    return jax.shard_map(
        on_device,
        mesh=mesh,
        in_specs=(
            P(("grp", "gx"), None, None),
            P(("grp", "gx"), None, None),
            P("gy", None, ("grp", "gx"), None, None),
            P("gy", None, ("grp", "gx"), None, None),
            P("gy", None, ("grp", "gx"), None),
            P(("grp", "gy")),
            P(("grp", "gx"), "gy", None),
            P(("grp", "gx"), "gy", None),
        ),
        out_specs=(
            P("gy", ("grp", "gx"), None, None),
            P(("grp", "gx"), "gy", None),
            P(("grp", "gx"), "gy", None),
        ),
        check_vma=False,
    )
```

time: 118 us -> 95.7 us (0.81)
  waiting for transfers between devices: 41.5 us -> 11.7 us
  local copies, waits for them, and re-layouts: 5.4 us -> 29.5 us
  starting transfers between devices: 44.2 us -> 21.1 us
  other arithmetic: 11.7 us -> 30.3 us
  between operations: 14.6 us -> 1.74 us
    reduce_scatter x1 -> x0, waiting for transfers between devices: 26.9 us -> none  [on_device(): lax.psum_scatter(grad_part, 'gy', scatter_dimension=1, tiled=True)]
    ppermute x16 -> x14, starting transfers between devices: 44.2 us -> 21.1 us  [the longest x5 17.4 us: to_outer(): return lax.ppermute(v, ('gx', 'gy'), outer_perm)]
    unnamed x18 -> x86, local copies, waits for them, and re-layouts: 2.96 us -> 12 us
    slice x7 -> x24, local copies, waits for them, and re-layouts: 0.89 us -> 7.46 us  [the longest x1 1.45 us: on_device(): saved_own = jnp.concatenate([saved[:, :, :own], saved_in], axis=0)]
    rev x0 -> x10, local copies, waits for them, and re-layouts: none -> 6.18 us  [the longest x2 2.95 us: on_device(): cur_inner = jnp.flip(i_in, 1)]
    concatenate x4 -> x13, other arithmetic: 0.33 us -> 6.19 us  [the longest x3 3.75 us: on_device(): curr_wide = jnp.concatenate([cur_outer, current, cur_inner], axis=1)]
    select_n x0 -> x7, other arithmetic: none -> 4.61 us  [the longest x5 4.58 us: orient(): return jnp.where(lower, v, jnp.flip(v, dim))]
    ppermute x16 -> x14, waiting for transfers between devices: 14.6 us -> 11.7 us  [the longest x5 8.13 us: to_outer(): return lax.ppermute(v, ('gx', 'gy'), outer_perm)]
  transfers between devices with their start and end apart: 17 -> 14, of which waited for: 9 -> 6; matrix products, arithmetic and copies ran while one was open for 2% -> 29% of each run, Pallas kernels for 0% -> 0%
where the time goes in v1:
time: 95.7 us; the launch traced here: 94.3 us
  other arithmetic  30.3 us (32%)
  local copies, waits for them, and re-layouts  29.5 us (31%)
  starting transfers between devices  21.1 us (22%)
  waiting for transfers between devices  11.7 us (12%)
  between operations  1.74 us (2%)
    ppermute x5, starting transfers between devices, to_outer(): return lax.ppermute(v, ('gx', 'gy'), outer_perm)  17.4 us
    unnamed x86, local copies, waits for them, and re-layouts  12 us
    ppermute x5, waiting for transfers between devices, to_outer(): return lax.ppermute(v, ('gx', 'gy'), outer_perm)  8.13 us
    select_n x5, other arithmetic, orient(): return jnp.where(lower, v, jnp.flip(v, dim))  4.58 us
    concatenate x3, other arithmetic, on_device(): curr_wide = jnp.concatenate([cur_outer, current, cur_inner], axis=1)  3.75 us
    rev x2, local copies, waits for them, and re-layouts, on_device(): cur_inner = jnp.flip(i_in, 1)  2.95 us
    ppermute x1, waiting for transfers between devices, on_device(): red = red + lax.ppermute(slice_of((pair + d) % pair_count), 'gy', perm)  2.93 us
    mul x6, other arithmetic, div_flux(): flow_z = face_z * (wave_pad[..., 1:] - wave_pad[..., :-1])  2.88 us
  transfers between devices with their start and end apart: 14, of which 6 were waited for; matrix products, arithmetic and copies ran while one was open for 29% of the time, Pallas kernels for 0%

profile of v1, /device:TPU:1, one launch (start us, length us, event | category | flops | bytes accessed | tf_op | source)
XLA Modules:
  0.0 94.3 jit_solution(18177241276315546819)
XLA Ops:
  0.6 1.7 %reverse_select_fusion.1 = f32[2,2,4,128,128]{4,3,2,1,0:T(8,128)S(1)} fusion(f32[2,2,4,128,128]{4,3,2,1,0:T(8,128)} %param.11, pred[]{:T(512)S(6)} %eq.19), kind=kLoop, calls=%fused_computation.30 | loop fusion | flops 262144 | bytes 2097153 | tf_op jit(solution)/shard_map/jit(_where)/select_n | solution.py:95
  2.4 0.7 slice_bitcast_fusion.3
  3.1 0.9 slice_bitcast_fusion.1
  4.3 1.1 %concatenate.103 = f16[1158,128]{1,0:T(8,128)(2,1)S(1)} concatenate(f16[774,128]{1,0:T(8,128)(2,1)S(1)} %fusion.65, f16[256,128]{1,0:T(8,128)(2,1)S(1)} %bitcast.126, f16[128,128]{1,0:T(8,128)(2,1)S(1)} %fusion.95), dimensions={0} | concatenate | bytes 592896 | tf_op jit(solution)/shard_map/concatenate | solution.py:126
  5.3 4.6 %collective-permute-start.2 = (f16[1158,128]{1,0:T(8,128)(2,1)S(1)}, f16[1158,128]{1,0:T(8,128)(2,1)S(1)}, u32[]{:S(2)}, u32[]{:S(2)}) collective-permute-start(f16[1158,128]{1,0:T(8,128)(2,1)S(1)} %concatenate.103), channel_id=1, source_target_pairs={{1,4},{4,1},{3,6},{6,3},{5,8},{8,5},{7,10},{10,7},{9,12},{12,9},{1... | collective-permute-start | bytes 889352 | tf_op jit(solution)/shard_map/ppermute | solution.py:89
  9.9 0.8 pad_maximum_fusion.7
  10.9 0.8 pad_maximum_fusion.2
  12.3 3.2 %copy.36 = bf16[2,8,4,128,128]{4,3,2,0,1:T(8,128)(2,1)} copy(bf16[2,8,4,128,128]{4,3,2,1,0:T(8,128)(2,1)} %param.10) | data formatting | bytes 4194304 | tf_op args[2]
  15.5 0.7 add_multiply_fusion.1
  16.1 0.9 fusion.78
  17.1 0.7 fusion.110
  18.1 0.6 copy-done.30
  18.9 1.6 %slice_multiply_fusion.1 = f32[2,128,128]{2,1,0:T(8,128)} fusion(f32[3,128,128]{2,1,0:T(8,128)} %copy-done.30), kind=kLoop, calls=%fused_computation.204 | loop fusion | flops 32768 | bytes 262144 | tf_op jit(solution)/shard_map/mul | solution.py:213
  20.5 1.0 %slice.737 = f32[512,128]{1,0:T(8,128)S(1)} slice(f32[768,128]{1,0:T(8,128)} %collective-permute-done.3), slice={[0:512], [0:128]} | slice | bytes 524288 | tf_op jit(solution)/shard_map/slice | solution.py:172
  21.5 0.7 rev.77
  22.2 0.9 slice.744
  23.1 0.7 maximum_bitcast_fusion
  23.8 0.7 slice.722
  24.6 1.1 %slice.719 = f32[1024,128]{1,0:T(8,128)S(1)} slice(f32[1074,128]{1,0:T(8,128)} %collective-permute-done), slice={[0:1024], [0:128]} | slice | bytes 1048576 | tf_op jit(solution)/shard_map/slice | solution.py:140
  25.7 0.8 slice_bitcast_fusion
  26.6 3.1 %collective-permute-start.1 = (f16[774,128]{1,0:T(8,128)(2,1)S(1)}, f16[774,128]{1,0:T(8,128)(2,1)S(1)}, u32[]{:S(2)}, u32[]{:S(2)}) collective-permute-start(f16[774,128]{1,0:T(8,128)(2,1)S(1)} %fusion.64), channel_id=1, source_target_pairs={{1,4},{4,1},{3,6},{6,3},{5,8},{8,5},{7,10},{10,7},{9,12},{12,9},{1... | collective-permute-start | bytes 594440 | tf_op jit(solution)/shard_map/ppermute | solution.py:89
  29.7 0.7 slice.769
  30.4 3.2 %collective-permute-done.1 = f16[774,128]{1,0:T(8,128)(2,1)S(1)} collective-permute-done((f16[774,128]{1,0:T(8,128)(2,1)S(1)}, f16[774,128]{1,0:T(8,128)(2,1)S(1)}, u32[]{:S(2)}, u32[]{:S(2)}) %collective-permute-start.1) | collective-permute-done | bytes 198176 | tf_op jit(solution)/shard_map/ppermute | solution.py:89
  33.7 0.7 copy-done.29
  34.5 1.1 %maximum_maximum_fusion = f32[4,6,128,128]{3,2,1,0:T(8,128)S(1)} fusion(f32[2,2,128,128]{3,2,1,0:T(8,128)} %rev.77, f32[2,2,128,128]{3,2,1,0:T(8,128)} %get-tuple-element.18, f32[2,2,128,128]{3,2,1,0:T(8,128)S(1)} %get-tuple-element.35, f32[2,2,128,128]{3,2,1,0:T(8,128)S(1)} %get-tuple-element.16, f32[4,2,128,128]{3,2,1,0:T(8,128)S(1)} %rev.76), kind=kLoop, calls=%fused_computation.27 | loop fusion | flops 1572864 | bytes 3145728 | tf_op jit(solution)/shard_map/concatenate | solution.py:199
  35.9 0.6 fusion.1
  36.7 0.7 slice-done.1
  37.7 0.9 fusion.28
  38.7 0.8 copy-done.7
  40.0 0.8 copy-done.18
  41.6 3.2 %collective-permute-start.4 = (f16[4,2,128,128]{3,2,1,0:T(8,128)(2,1)S(1)}, f16[4,2,128,128]{3,2,1,0:T(8,128)(2,1)S(1)}, u32[]{:S(2)}, u32[]{:S(2)}) collective-permute-start(f16[4,2,128,128]{3,2,1,0:T(8,128)(2,1)S(1)} %get-tuple-element.30), channel_id=1, source_target_pairs={{1,4},{4,1},{3,6},{6,3},{5,8},{8,5},{7,10},{10,7},{9,12},{12,9},{1... | collective-permute-start | bytes 786440 | tf_op jit(solution)/shard_map/ppermute | solution.py:89
  44.9 2.0 %reverse_select_fusion = bf16[2,8,4,128,128]{4,3,2,0,1:T(8,128)(2,1)} fusion(bf16[2,8,4,128,128]{4,3,2,0,1:T(8,128)(2,1)S(1)} %copy-done.3, pred[]{:T(512)S(6)} %eq.19), kind=kLoop, calls=%fused_computation.14 | loop fusion | flops 1048576 | bytes 4194305 | tf_op jit(solution)/shard_map/jit(_where)/select_n | solution.py:95
  46.9 2.5 %collective-permute-done.4 = f16[4,2,128,128]{3,2,1,0:T(8,128)(2,1)S(1)} collective-permute-done((f16[4,2,128,128]{3,2,1,0:T(8,128)(2,1)S(1)}, f16[4,2,128,128]{3,2,1,0:T(8,128)(2,1)S(1)}, u32[]{:S(2)}, u32[]{:S(2)}) %collective-permute-start.4) | collective-permute-done | bytes 262176 | tf_op jit(solution)/shard_map/ppermute | solution.py:89
  49.4 0.8 reverse_multiply_fusion.1
  50.3 1.1 %rev.80 = f32[4,2,128,128]{3,2,1,0:T(8,128)S(1)} reverse(f32[4,2,128,128]{3,2,1,0:T(8,128)} %collective-permute-done.5), dimensions={1} | reverse | bytes 1048576 | tf_op jit(solution)/shard_map/jit(_flip)/rev | solution.py:198
  51.3 1.1 %pad_maximum_fusion = f32[4,6,128,128]{3,2,1,0:T(8,128)S(1)} fusion(f32[4,2,128,128]{3,2,1,0:T(8,128)S(1)} %rev.80, f32[4,2,128,128]{3,2,1,0:T(8,128)S(1)} %fusion.62, f32[4,2,128,128]{3,2,1,0:T(8,128)} %reverse_multiply_fusion.1), kind=kLoop, calls=%fused_computation.28 | loop fusion | flops 786432 | bytes 3145728 | tf_op jit(solution)/shard_map/concatenate | solution.py:199
  52.7 0.6 fusion.3
  53.5 0.8 copy-done.11
  54.3 0.8 fusion.23
  55.3 0.8 copy-done.8
  56.5 0.8 copy-done.25
  57.9 0.9 %multiply_convert_fusion = (f16[4,2,128,128]{3,2,1,0:T(8,128)(2,1)}, f32[4,2,128,128]{3,2,1,0:T(8,128)}) fusion(f32[2,2,128,128]{3,2,1,0:T(8,128)S(1)} %get-tuple-element.29, f32[2,2,128,128]{3,2,1,0:T(8,128)S(1)} %get-tuple-element.28), kind=kLoop, calls=%fused_computation.156 | loop fusion | flops 393216 | bytes 1310720 | tf_op jit(solution)/shard_map/convert_element_type | solution.py:195
  58.8 3.4 %collective-permute-start.6 = (f16[4,2,128,128]{3,2,1,0:T(8,128)(2,1)}, f16[4,2,128,128]{3,2,1,0:T(8,128)(2,1)}, u32[]{:S(2)}, u32[]{:S(2)}) collective-permute-start(f16[4,2,128,128]{3,2,1,0:T(8,128)(2,1)} %get-tuple-element.26), channel_id=1, source_target_pairs={{1,4},{4,1},{3,6},{6,3},{5,8},{8,5},{7,10},{10,7},{9,12},{12,9},{1... | collective-permute-start | bytes 786440 | tf_op jit(solution)/shard_map/ppermute | solution.py:89
  62.3 1.5 %fusion.109 = (bf16[2,8,2,128,128]{4,3,2,0,1:T(8,128)(2,1)}, bf16[2,8,2,128,128]{4,3,2,0,1:T(8,128)(2,1)}) fusion(bf16[2,8,4,128,128]{4,3,2,0,1:T(8,128)(2,1)S(1)} %copy-done.4), kind=kLoop, calls=%fused_computation.268 | loop fusion | bytes 4194304 | tf_op jit(solution)/shard_map/slice | solution.py:183
  63.8 2.3 %rev.86 = bf16[2,8,2,128,128]{4,3,2,0,1:T(8,128)(2,1)} reverse(bf16[2,8,2,128,128]{4,3,2,0,1:T(8,128)(2,1)} %get-tuple-element.12), dimensions={2} | reverse | bytes 2097152 | tf_op jit(solution)/shard_map/jit(_flip)/rev | solution.py:137
  66.9 1.0 %convert_element_type.147 = f32[4,2,128,128]{3,2,1,0:T(8,128)S(1)} convert(f16[4,2,128,128]{3,2,1,0:T(8,128)(2,1)} %collective-permute-done.6) | non-fusion elementwise | flops 131072 | bytes 786432 | tf_op jit(solution)/shard_map/convert_element_type | solution.py:197
  67.9 0.9 reverse_multiply_fusion
  68.8 1.9 %rev.82 = f32[4,2,128,128]{3,2,1,0:T(8,128)} reverse(f32[4,2,128,128]{3,2,1,0:T(8,128)} %collective-permute-done.7), dimensions={1} | reverse | bytes 1048576 | tf_op jit(solution)/shard_map/jit(_flip)/rev | solution.py:198
  70.7 1.5 %pad_maximum_fusion.1 = f32[4,6,128,128]{3,2,1,0:T(8,128)S(1)} fusion(f32[4,2,128,128]{3,2,1,0:T(8,128)} %rev.82, f32[4,2,128,128]{3,2,1,0:T(8,128)} %copy-done.1, f32[4,2,128,128]{3,2,1,0:T(8,128)} %reverse_multiply_fusion), kind=kLoop, calls=%fused_computation.29 | loop fusion | flops 786432 | bytes 3145728 | tf_op jit(solution)/shard_map/concatenate | solution.py:199
  72.2 0.6 fusion.5
  73.5 0.8 copy-done.12
  74.3 0.8 fusion.18
  75.3 1.1 %copy-done = bf16[2,8,2,128,128]{4,3,2,0,1:T(8,128)(2,1)S(1)} copy-done((bf16[2,8,2,128,128]{4,3,2,0,1:T(8,128)(2,1)S(1)}, bf16[2,8,2,128,128]{4,3,2,0,1:T(8,128)(2,1)}, u32[]{:S(2)}) %copy-start) | copy-done | bytes 1048600
  76.4 1.3 %fusion.37 = (f32[2,128,128]{2,1,0:T(8,128)S(1)}, f32[4,2,128,128]{3,2,1,0:T(8,128)S(1)}) fusion(f32[4,4,128,128]{3,2,1,0:T(8,128)S(1)} %fusion.18, bf16[2,8,2,128,128]{4,3,2,0,1:T(8,128)(2,1)} %collective-permute-done.9, bf16[2,8,2,128,128]{4,3,2,0,1:T(8,128)(2,1)S(1)} %copy-done), kind=kLoop, calls=%fused_computation.114 | loop fusion | flops 1409024 | bytes 3276800 | tf_op jit(solution)/shard_map/reduce_sum | solution.py:215
  78.2 0.6 copy-done.2
  78.8 2.4 %fusion.41 = (f32[2,128,128]{2,1,0:T(8,128)S(1)}, f32[2,128,128]{2,1,0:T(8,128)S(1)}, f32[2,128,128]{2,1,0:T(8,128)S(1)}, f32[2,128,128]{2,1,0:T(8,128)S(1)}, f3...) fusion(f32[4,2,128,128]{3,2,1,0:T(8,128)S(1)} %fusion.62, ...), kind=kLoop, calls=%fused_computation.118 | loop fusion | flops 8486912 | bytes 9181184 | tf_op jit(solution)/shard_map/reduce_sum | solution.py:218
  81.3 1.3 %collective-permute-start.10 = (f32[2,66,128]{2,1,0:T(8,128)S(1)}, f32[2,66,128]{2,1,0:T(8,128)S(1)}, u32[]{:S(2)}, u32[]{:S(2)}) collective-permute-start(f32[2,66,128]{2,1,0:T(8,128)S(1)} %fusion.94), channel_id=1, source_target_pairs={{0,2},{1,3},{2,0},{3,1},{4,6},{5,7},{6,4},{7,5},{8,10},{9,11},{10,... | collective-permute-start | bytes 202760 | tf_op jit(solution)/shard_map/ppermute | solution.py:247
  82.6 2.9 %collective-permute-done.10 = f32[2,66,128]{2,1,0:T(8,128)S(1)} collective-permute-done((f32[2,66,128]{2,1,0:T(8,128)S(1)}, f32[2,66,128]{2,1,0:T(8,128)S(1)}, u32[]{:S(2)}, u32[]{:S(2)}) %collective-permute-start.10) | collective-permute-done | bytes 67616 | tf_op jit(solution)/shard_map/ppermute | solution.py:247
  85.5 0.6 collective-permute-start.11
  86.1 3.1 %collective-permute-start.12 = (f32[1,64,128]{2,1,0:T(8,128)S(1)}, f32[1,64,128]{2,1,0:T(8,128)S(1)}, u32[]{:S(2)}, u32[]{:S(2)}) collective-permute-start(f32[1,64,128]{2,1,0:T(8,128)S(1)} %get-tuple-element.42), channel_id=1, source_target_pairs={{1,4},{4,1},{3,6},{6,3},{5,8},{8,5},{7,10},{10,7},{9,12},{12,9},{1... | collective-permute-start | bytes 98312 | tf_op jit(solution)/shard_map/ppermute | solution.py:89
  89.3 2.1 %collective-permute-done.12 = f32[1,64,128]{2,1,0:T(8,128)S(1)} collective-permute-done((f32[1,64,128]{2,1,0:T(8,128)S(1)}, f32[1,64,128]{2,1,0:T(8,128)S(1)}, u32[]{:S(2)}, u32[]{:S(2)}) %collective-permute-start.12) | collective-permute-done | bytes 32800 | tf_op jit(solution)/shard_map/ppermute | solution.py:89
  92.1 0.6 collective-permute-done.13
  92.7 0.7 multiply_subtract_fusion
  93.5 0.8 reverse_select_fusion.2
  (180 shorter events, 8.3 us)
Async XLA Ops:
  2.3 1.6 %copy-start.39 = (bf16[2,6,4,128]{3,2,1,0:T(4,128)(2,1)S(1)}, bf16[2,6,4,128]{3,2,1,0:T(4,128)(2,1)}, u32[]{:S(2)}) copy-start(bf16[2,6,4,128]{3,2,1,0:T(4,128)(2,1)} %param.12) | copy-start | bytes 36868
  2.4 1.7 %copy-start.36 = (f32[4,128,128]{2,1,0:T(8,128)S(1)}, f32[4,128,128]{2,1,0:T(8,128)}, u32[]{:S(2)}) copy-start(f32[4,128,128]{2,1,0:T(8,128)} %param.9) | copy-start | bytes 786436
  3.1 1.1 %copy-start.37 = (f32[4,128,128]{2,1,0:T(8,128)S(1)}, f32[4,128,128]{2,1,0:T(8,128)}, u32[]{:S(2)}) copy-start(f32[4,128,128]{2,1,0:T(8,128)} %param.8) | copy-start | bytes 786436
  4.0 30.5 %copy-start.17 = (f32[2,2,128,128]{3,2,1,0:T(8,128)}, f32[2,2,128,128]{3,2,1,0:T(8,128)S(1)}, u32[]{:S(2)}) copy-start(f32[2,2,128,128]{3,2,1,0:T(8,128)S(1)} %get-tuple-element.16) | copy-start | bytes 786436
  4.2 13.7 %copy-start.27 = (f32[4,128,128]{2,1,0:T(8,128)}, f32[4,128,128]{2,1,0:T(8,128)S(1)}, u32[]{:S(2)}) copy-start(f32[4,128,128]{2,1,0:T(8,128)S(1)} %reverse_select_fusion.3) | copy-start | bytes 786436
  4.2 6.6 %copy-start.41 = (s32[2]{0:T(128)S(1)}, s32[2]{0:T(128)}, u32[]{:S(2)}) copy-start(s32[2]{0:T(128)} %param.13) | copy-start | bytes 28
  5.3 11.7 %collective-permute-start.2 = (f16[1158,128]{1,0:T(8,128)(2,1)S(1)}, f16[1158,128]{1,0:T(8,128)(2,1)S(1)}, u32[]{:S(2)}, u32[]{:S(2)}) collective-permute-start(f16[1158,128]{1,0:T(8,128)(2,1)S(1)} %concatenate.103), channel_id=1, source_target_pairs={{1,4},{4,1},{3,6},{6,3},{5,8},{8,5},{7,10},{10,7},{9,12},{12,9},{1... | collective-permute-start | bytes 889352 | tf_op jit(solution)/shard_map/ppermute | solution.py:89
  10.7 9.8 %collective-permute-start.3 = (f32[768,128]{1,0:T(8,128)}, f32[768,128]{1,0:T(8,128)}, u32[]{:S(2)}, u32[]{:S(2)}) collective-permute-start(f32[768,128]{1,0:T(8,128)} %pad_maximum_fusion.7), channel_id=1, source_target_pairs={{0,1},{1,0},{2,3},{3,2},{4,5},{5,4},{6,7},{7,6},{8,9},{9,8},{10,11... | collective-permute-start | bytes 1179656 | tf_op jit(solution)/shard_map/ppermute | solution.py:92
  11.8 12.1 %collective-permute-start = (f32[1074,128]{1,0:T(8,128)}, f32[1074,128]{1,0:T(8,128)}, u32[]{:S(2)}, u32[]{:S(2)}) collective-permute-start(f32[1074,128]{1,0:T(8,128)} %pad_maximum_fusion.2), channel_id=1, source_target_pairs={{0,1},{1,0},{2,3},{3,2},{4,5},{5,4},{6,7},{7,6},{8,9},{9,8},{10,11... | collective-permute-start | bytes 1649672 | tf_op jit(solution)/shard_map/ppermute | solution.py:92
  17.1 1.7 %copy-start.16 = (f32[1158,128]{1,0:T(8,128)}, f32[1158,128]{1,0:T(8,128)S(1)}, u32[]{:S(2)}) copy-start(f32[1158,128]{1,0:T(8,128)S(1)} %convert_multiply_fusion.6) | copy-start | bytes 1778692
  18.0 0.7 copy-start.30
  18.0 21.9 %copy-start.13 = (f32[3,128,128]{2,1,0:T(8,128)}, f32[3,128,128]{2,1,0:T(8,128)S(1)}, u32[]{:S(2)}) copy-start(f32[3,128,128]{2,1,0:T(8,128)S(1)} %get-tuple-element.37) | copy-start | bytes 589828
  18.0 34.5 %copy-start.5 = (f32[4,129,128]{2,1,0:T(8,128)}, f32[4,129,128]{2,1,0:T(8,128)S(1)}, u32[]{:S(2)}) copy-start(f32[4,129,128]{2,1,0:T(8,128)S(1)} %add_multiply_fusion) | copy-start | bytes 792580
  18.7 18.0 %copy-start.10 = (f32[4,128,128]{2,1,0:T(8,128)}, f32[4,128,128]{2,1,0:T(8,128)S(1)}, u32[]{:S(2)}) copy-start(f32[4,128,128]{2,1,0:T(8,128)S(1)} %maximum_multiply_fusion.2) | copy-start | bytes 786436
  18.7 4.4 %copy-start.35 = (f32[2,1,128,128]{3,2,0,1:T(8,128)S(1)}, f32[2,1,128,128]{3,2,0,1:T(8,128)}, u32[]{:S(2)}) copy-start(f32[2,1,128,128]{3,2,0,1:T(8,128)} %get-tuple-element.19) | copy-start | bytes 393220
  25.7 8.7 %slice-start = ((f32[1158,128]{1,0:T(8,128)}), f32[512,128]{1,0:T(8,128)S(1)}, s32[]{:S(2)}) async-start(f32[1158,128]{1,0:T(8,128)} %copy-done.16), calls=%async_computation | async-start | bytes 524288 | tf_op jit(solution)/shard_map/slice | solution.py:152
  26.5 8.0 %copy-start.19 = (f32[2,2,128,128]{3,2,1,0:T(8,128)}, f32[2,2,128,128]{3,2,1,0:T(8,128)S(1)}, u32[]{:S(2)}) copy-start(f32[2,2,128,128]{3,2,1,0:T(8,128)S(1)} %get-tuple-element.35) | copy-start | bytes 786436
  26.6 7.0 %collective-permute-start.1 = (f16[774,128]{1,0:T(8,128)(2,1)S(1)}, f16[774,128]{1,0:T(8,128)(2,1)S(1)}, u32[]{:S(2)}, u32[]{:S(2)}) collective-permute-start(f16[774,128]{1,0:T(8,128)(2,1)S(1)} %fusion.64), channel_id=1, source_target_pairs={{1,4},{4,1},{3,6},{6,3},{5,8},{8,5},{7,10},{10,7},{9,12},{12,9},{1... | collective-permute-start | bytes 594440 | tf_op jit(solution)/shard_map/ppermute | solution.py:89
  33.6 0.8 copy-start.29
  36.5 0.9 slice-start.1
  36.5 1.0 %copy-start.31 = (f32[2,2,128,128]{3,2,1,0:T(8,128)S(1)}, f32[2,2,128,128]{3,2,1,0:T(8,128)}, u32[]{:S(2)}) copy-start(f32[2,2,128,128]{3,2,1,0:T(8,128)} %get-tuple-element.15) | copy-start | bytes 786436
  36.5 1.1 %copy-start.32 = (f32[2,2,128,128]{3,2,1,0:T(8,128)S(1)}, f32[2,2,128,128]{3,2,1,0:T(8,128)}, u32[]{:S(2)}) copy-start(f32[2,2,128,128]{3,2,1,0:T(8,128)} %get-tuple-element.34) | copy-start | bytes 786436
  36.5 1.2 %copy-start.33 = (f32[4,1,128,128]{3,2,1,0:T(8,128)S(1)}, f32[4,1,128,128]{3,2,1,0:T(8,128)}, u32[]{:S(2)}) copy-start(f32[4,1,128,128]{3,2,1,0:T(8,128)} %maximum_bitcast_fusion) | copy-start | bytes 786436
  36.5 1.2 %copy-start.34 = (f32[256,128]{1,0:T(8,128)S(1)}, f32[256,128]{1,0:T(8,128)}, u32[]{:S(2)}) copy-start(f32[256,128]{1,0:T(8,128)} %get-tuple-element.22) | copy-start | bytes 393220
  37.7 0.9 %copy-start.21 = (f32[2,129,128]{2,1,0:T(8,128)S(1)}, f32[2,129,128]{2,1,0:T(8,128)}, u32[]{:S(2)}) copy-start(f32[2,129,128]{2,1,0:T(8,128)} %add_multiply_fusion.1) | copy-start | bytes 396292
  38.6 1.0 %copy-start.7 = (f32[2,128,129]{2,1,0:T(8,128)S(1)}, f32[2,128,129]{2,1,0:T(8,128)}, u32[]{:S(2)}) copy-start(f32[2,128,129]{2,1,0:T(8,128)} %fusion.78) | copy-start | bytes 396292
  39.9 1.0 %copy-start.18 = (f32[2,2,128,128]{3,2,1,0:T(8,128)S(1)}, f32[2,2,128,128]{3,2,1,0:T(8,128)}, u32[]{:S(2)}) copy-start(f32[2,2,128,128]{3,2,1,0:T(8,128)} %copy-done.17) | copy-start | bytes 786436
  39.9 1.0 %copy-start.20 = (f32[2,2,128,128]{3,2,1,0:T(8,128)S(1)}, f32[2,2,128,128]{3,2,1,0:T(8,128)}, u32[]{:S(2)}) copy-start(f32[2,2,128,128]{3,2,1,0:T(8,128)} %copy-done.19) | copy-start | bytes 786436
  39.9 1.0 %copy-start.24 = (f32[2,128,128]{2,1,0:T(8,128)S(1)}, f32[2,128,128]{2,1,0:T(8,128)}, u32[]{:S(2)}) copy-start(f32[2,128,128]{2,1,0:T(8,128)} %slice_multiply_fusion.1) | copy-start | bytes 393220
  41.4 3.5 %copy-start.3 = (bf16[2,8,4,128,128]{4,3,2,0,1:T(8,128)(2,1)S(1)}, bf16[2,8,4,128,128]{4,3,2,0,1:T(8,128)(2,1)}, u32[]{:S(2)}) copy-start(bf16[2,8,4,128,128]{4,3,2,0,1:T(8,128)(2,1)} %copy.36) | copy-start | bytes 6291460
  41.6 7.8 %collective-permute-start.4 = (f16[4,2,128,128]{3,2,1,0:T(8,128)(2,1)S(1)}, f16[4,2,128,128]{3,2,1,0:T(8,128)(2,1)S(1)}, u32[]{:S(2)}, u32[]{:S(2)}) collective-permute-start(f16[4,2,128,128]{3,2,1,0:T(8,128)(2,1)S(1)} %get-tuple-element.30), channel_id=1, source_target_pairs={{1,4},{4,1},{3,6},{6,3},{5,8},{8,5},{7,10},{10,7},{9,12},{12,9},{1... | collective-permute-start | bytes 786440 | tf_op jit(solution)/shard_map/ppermute | solution.py:89
  44.8 5.5 %collective-permute-start.5 = (f32[4,2,128,128]{3,2,1,0:T(8,128)S(1)}, f32[4,2,128,128]{3,2,1,0:T(8,128)}, u32[]{:S(2)}, u32[]{:S(2)}) collective-permute-start(f32[4,2,128,128]{3,2,1,0:T(8,128)S(1)} %get-tuple-element.31), channel_id=1, source_target_pairs={{0,1},{1,0},{2,3},{3,2},{4,5},{5,4},{6,7},{7,6},{8,9},{9,8},{10,11... | collective-permute-start | bytes 1572872 | tf_op jit(solution)/shard_map/ppermute | solution.py:92
  53.4 1.0 %copy-start.11 = (f32[4,128,128]{2,1,0:T(8,128)S(1)}, f32[4,128,128]{2,1,0:T(8,128)}, u32[]{:S(2)}) copy-start(f32[4,128,128]{2,1,0:T(8,128)} %copy-done.10) | copy-start | bytes 786436
  54.3 0.9 copy-start.22
  55.1 1.0 %copy-start.8 = (f32[2,128,129]{2,1,0:T(8,128)S(1)}, f32[2,128,129]{2,1,0:T(8,128)}, u32[]{:S(2)}) copy-start(f32[2,128,129]{2,1,0:T(8,128)} %fusion.78) | copy-start | bytes 396292
  55.2 1.2 %copy-start.14 = (f32[3,128,128]{2,1,0:T(8,128)S(1)}, f32[3,128,128]{2,1,0:T(8,128)}, u32[]{:S(2)}) copy-start(f32[3,128,128]{2,1,0:T(8,128)} %copy-done.13) | copy-start | bytes 589828
  56.4 0.9 copy-start.25
  57.8 6.0 %copy-start.1 = (f32[4,2,128,128]{3,2,1,0:T(8,128)}, f32[4,2,128,128]{3,2,1,0:T(8,128)S(1)}, u32[]{:S(2)}) copy-start(f32[4,2,128,128]{3,2,1,0:T(8,128)S(1)} %fusion.57) | copy-start | bytes 1572868
  57.8 4.5 %copy-start.4 = (bf16[2,8,4,128,128]{4,3,2,0,1:T(8,128)(2,1)S(1)}, bf16[2,8,4,128,128]{4,3,2,0,1:T(8,128)(2,1)}, u32[]{:S(2)}) copy-start(bf16[2,8,4,128,128]{4,3,2,0,1:T(8,128)(2,1)} %reverse_select_fusion) | copy-start | bytes 6291460
  58.8 8.1 %collective-permute-start.6 = (f16[4,2,128,128]{3,2,1,0:T(8,128)(2,1)}, f16[4,2,128,128]{3,2,1,0:T(8,128)(2,1)}, u32[]{:S(2)}, u32[]{:S(2)}) collective-permute-start(f16[4,2,128,128]{3,2,1,0:T(8,128)(2,1)} %get-tuple-element.26), channel_id=1, source_target_pairs={{1,4},{4,1},{3,6},{6,3},{5,8},{8,5},{7,10},{10,7},{9,12},{12,9},{1... | collective-permute-start | bytes 786440 | tf_op jit(solution)/shard_map/ppermute | solution.py:89
  62.2 6.6 %collective-permute-start.7 = (f32[4,2,128,128]{3,2,1,0:T(8,128)}, f32[4,2,128,128]{3,2,1,0:T(8,128)}, u32[]{:S(2)}, u32[]{:S(2)}) collective-permute-start(f32[4,2,128,128]{3,2,1,0:T(8,128)} %get-tuple-element.27), channel_id=1, source_target_pairs={{0,1},{1,0},{2,3},{3,2},{4,5},{5,4},{6,7},{7,6},{8,9},{9,8},{10,11... | collective-permute-start | bytes 1572872 | tf_op jit(solution)/shard_map/ppermute | solution.py:92
  66.1 9.2 %collective-permute-start.9 = (bf16[2,8,2,128,128]{4,3,2,0,1:T(8,128)(2,1)}, bf16[2,8,2,128,128]{4,3,2,0,1:T(8,128)(2,1)}, u32[]{:S(2)}, u32[]{:S(2)}) collective-permute-start(bf16[2,8,2,128,128]{4,3,2,0,1:T(8,128)(2,1)} %rev.86), channel_id=1, source_target_pairs={{0,1},{1,0},{2,3},{3,2},{4,5},{5,4},{6,7},{7,6},{8,9},{9,8},{10,11... | collective-permute-start | bytes 3145736 | tf_op jit(solution)/shard_map/ppermute | solution.py:92
  72.2 1.0 %copy-start.6 = (f32[4,129,128]{2,1,0:T(8,128)S(1)}, f32[4,129,128]{2,1,0:T(8,128)}, u32[]{:S(2)}) copy-start(f32[4,129,128]{2,1,0:T(8,128)} %copy-done.5) | copy-start | bytes 792580
  73.3 1.0 %copy-start.12 = (f32[4,128,128]{2,1,0:T(8,128)S(1)}, f32[4,128,128]{2,1,0:T(8,128)}, u32[]{:S(2)}) copy-start(f32[4,128,128]{2,1,0:T(8,128)} %copy-done.10) | copy-start | bytes 786436
  74.3 0.9 copy-start.15
  75.2 1.2 %copy-start = (bf16[2,8,2,128,128]{4,3,2,0,1:T(8,128)(2,1)S(1)}, bf16[2,8,2,128,128]{4,3,2,0,1:T(8,128)(2,1)}, u32[]{:S(2)}) copy-start(bf16[2,8,2,128,128]{4,3,2,0,1:T(8,128)(2,1)} %get-tuple-element.11) | copy-start | bytes 3145732
  76.4 1.3 %copy-start.23 = (f32[2,129,128]{2,1,0:T(8,128)S(1)}, f32[2,129,128]{2,1,0:T(8,128)}, u32[]{:S(2)}) copy-start(f32[2,129,128]{2,1,0:T(8,128)} %add_multiply_fusion.1) | copy-start | bytes 396292
  76.4 1.4 %copy-start.9 = (f32[2,128,129]{2,1,0:T(8,128)S(1)}, f32[2,128,129]{2,1,0:T(8,128)}, u32[]{:S(2)}) copy-start(f32[2,128,129]{2,1,0:T(8,128)} %fusion.78) | copy-start | bytes 396292
  77.7 1.0 %copy-start.2 = (f32[4,2,128,128]{3,2,1,0:T(8,128)S(1)}, f32[4,2,128,128]{3,2,1,0:T(8,128)}, u32[]{:S(2)}) copy-start(f32[4,2,128,128]{3,2,1,0:T(8,128)} %copy-done.1) | copy-start | bytes 1572868
  77.7 1.1 %copy-start.26 = (f32[2,128,128]{2,1,0:T(8,128)S(1)}, f32[2,128,128]{2,1,0:T(8,128)}, u32[]{:S(2)}) copy-start(f32[2,128,128]{2,1,0:T(8,128)} %slice_multiply_fusion.1) | copy-start | bytes 393220
  78.8 2.4 %copy-start.28 = (f32[4,128,128]{2,1,0:T(8,128)S(1)}, f32[4,128,128]{2,1,0:T(8,128)}, u32[]{:S(2)}) copy-start(f32[4,128,128]{2,1,0:T(8,128)} %copy-done.27) | copy-start | bytes 786436
  81.2 11.5 %copy-start.38 = (f32[4,32,128]{2,1,0:T(8,128)S(1)}, f32[4,32,128]{2,1,0:T(8,128)}, u32[]{:S(2)}) copy-start(f32[4,32,128]{2,1,0:T(8,128)} %param.14) | copy-start | bytes 196612
  81.2 11.5 %copy-start.40 = (bf16[4,32,128]{2,1,0:T(8,128)(2,1)S(1)}, bf16[4,32,128]{2,1,0:T(8,128)(2,1)}, u32[]{:S(2)}) copy-start(bf16[4,32,128]{2,1,0:T(8,128)(2,1)} %param.15) | copy-start | bytes 98308
  81.3 4.2 %collective-permute-start.10 = (f32[2,66,128]{2,1,0:T(8,128)S(1)}, f32[2,66,128]{2,1,0:T(8,128)S(1)}, u32[]{:S(2)}, u32[]{:S(2)}) collective-permute-start(f32[2,66,128]{2,1,0:T(8,128)S(1)} %fusion.94), channel_id=1, source_target_pairs={{0,2},{1,3},{2,0},{3,1},{4,6},{5,7},{6,4},{7,5},{8,10},{9,11},{10,... | collective-permute-start | bytes 202760 | tf_op jit(solution)/shard_map/ppermute | solution.py:247
  85.5 3.7 %collective-permute-start.11 = (f32[1,64,128]{2,1,0:T(8,128)S(1)}, f32[1,64,128]{2,1,0:T(8,128)S(1)}, u32[]{:S(2)}, u32[]{:S(2)}) collective-permute-start(f32[1,64,128]{2,1,0:T(8,128)S(1)} %get-tuple-element.41), channel_id=1, source_target_pairs={{0,1},{1,0},{2,3},{3,2},{4,5},{5,4},{6,7},{7,6},{8,9},{9,8},{10,11... | collective-permute-start | bytes 98312 | tf_op jit(solution)/shard_map/ppermute | solution.py:92
  86.1 5.2 %collective-permute-start.12 = (f32[1,64,128]{2,1,0:T(8,128)S(1)}, f32[1,64,128]{2,1,0:T(8,128)S(1)}, u32[]{:S(2)}, u32[]{:S(2)}) collective-permute-start(f32[1,64,128]{2,1,0:T(8,128)S(1)} %get-tuple-element.42), channel_id=1, source_target_pairs={{1,4},{4,1},{3,6},{6,3},{5,8},{8,5},{7,10},{10,7},{9,12},{12,9},{1... | collective-permute-start | bytes 98312 | tf_op jit(solution)/shard_map/ppermute | solution.py:89
  91.4 1.3 %collective-permute-start.13 = (f32[2,32,128]{2,1,0:T(8,128)S(1)}, f32[2,32,128]{2,1,0:T(8,128)S(1)}, u32[]{:S(2)}, u32[]{:S(2)}) collective-permute-start(f32[2,32,128]{2,1,0:T(8,128)S(1)} %get-tuple-element.44), channel_id=1, source_target_pairs={{0,1},{1,0},{2,3},{3,2},{4,5},{5,4},{6,7},{7,6},{8,9},{9,8},{10,11... | collective-permute-start | bytes 98312 | tf_op jit(solution)/shard_map/ppermute | solution.py:92
  91.5 1.9 %collective-permute-start.8 = (f32[2,2,128,128]{3,2,1,0:T(8,128)S(1)}, f32[2,2,128,128]{3,2,1,0:T(8,128)S(1)}, u32[]{:S(2)}, u32[]{:S(2)}) collective-permute-start(f32[2,2,128,128]{3,2,1,0:T(8,128)S(1)} %get-tuple-element.25), channel_id=1, source_target_pairs={{0,1},{1,0},{2,3},{3,2},{4,5},{5,4},{6,7},{7,6},{8,9},{9,8},{10,11... | collective-permute-start | bytes 786440 | tf_op jit(solution)/shard_map/ppermute | solution.py:92

commit v2 on v0

v2 whole, which is shorter than its diff:
```python
import functools

import jax
import jax.numpy as jnp
from jax import lax
from jax.experimental import pallas as pl
from jax.experimental.pallas import tpu as pltpu
from jax.sharding import PartitionSpec as P

time_square = 0.2
WIRE = jnp.float16
F32 = jnp.float32
VMEM_LIMIT = 20 << 20
BLOCK = 16


def field_bounds(steps_count):
    bounds = [6.0, 6.0]
    for _ in range(steps_count):
        bounds.append(2.0 * bounds[-1] + bounds[-2] + time_square * 2.0 * 6.0)
    return bounds[1:]


def wire_scale(bound):
    scale = 1.0
    while scale * 2.0 * bound < 65000.0:
        scale = scale * 2.0
    return scale


def call(body, outs, *args, flops=1e6, name=None):
    spec = pl.BlockSpec(memory_space=pltpu.VMEM)
    return pl.pallas_call(
        body,
        out_shape=tuple(jax.ShapeDtypeStruct(s, F32) for s in outs),
        in_specs=[spec] * len(args),
        out_specs=(spec,) * len(outs),
        compiler_params=pltpu.CompilerParams(vmem_limit_bytes=VMEM_LIMIT),
        cost_estimate=pl.CostEstimate(flops=int(flops), bytes_accessed=4 << 20, transcendentals=0),
        name=name,
    )(*args)


def native(j, layers):
    return j + (lax.axis_index("gy") % 2) * (layers - 1 - 2 * j)


def spot(column, hot):
    return jnp.where(hot > 0.5, column, 0.0)


def payload_body(steps, scale, adj, buoy, slow, cols, hots, rows, out_a, out_b):
    shots, _, layers, ny, nz = adj.shape
    own = layers // 2
    for half, out in ((0, out_a), (1, out_b)):
        at = 0
        js = [0, 1] if half == 0 else [layers - 1, layers - 2]
        for s in range(shots):
            for j in js[:own]:
                out[at : at + ny, :] = adj[s, 1, native(j, layers)] * scale
                at += ny
        j = js[0]
        n = native(j, layers)
        mod = time_square / (buoy[n] * slow[n] * slow[n])
        for s in range(shots):
            c = (s * steps) * layers + j
            src = spot(cols[:, c : c + 1], hots[s : s + 1, :])
            out[at : at + ny, :] = (adj[s, 0, n] - mod * src) * scale
            at += ny
        if half == 0:
            for j in js:
                out[at : at + ny, :] = (buoy[native(j, layers)] - 0.75) * scale
                at += ny
            out[at : at + ny, :] = (slow[native(0, layers)] - 1.5) * scale
            at += ny
        out[at:, :] = rows[16 * half : 16 * half + 16, :] * scale


def prepare_body(
    steps, adj, adj_in, buoy, slow, wire_a, cols, hots, valid, cur, inner, co, cs, p_out, q_out
):
    shots, _, layers, ny, nz = adj.shape
    own = layers // 2
    both = 2 * shots
    for s in range(both):
        ref = adj if s < shots else adj_in
        w = (s + shots) % both
        for j in range(own):
            cur[s, j] = ref[s % shots, 1, native(j, layers)]
            inner[w, j] = ref[s % shots, 1, native(layers - 1 - j, layers)]
    base = 3 * shots * ny
    lane = lax.broadcasted_iota(jnp.int32, (BLOCK, nz), 1)
    left = lane > 0
    right = lane < nz - 1
    ok = valid[0:1, :]
    for y0 in range(0, ny, BLOCK):
        ys = slice(y0, y0 + BLOCK)
        b = []
        for d in (1, 0):
            b.append((wire_a[base + d * ny + y0 : base + d * ny + y0 + BLOCK, :] + 0.75) * ok)
        for j in range(own + 2):
            b.append(buoy[native(j, layers), ys, :])
        row = lax.broadcasted_iota(jnp.int32, (BLOCK, nz), 0) + y0
        for j in range(-1, own + 1):
            c = b[j + 2]
            if j < 0:
                sl = wire_a[base + 2 * ny + y0 : base + 2 * ny + y0 + BLOCK, :] + 1.5
                mod = ok * (time_square / (jnp.maximum(c, 0.5) * sl * sl))
                n = None
            else:
                n = native(j, layers)
                sl = slow[n, ys, :]
                mod = time_square / (c * sl * sl)
            if n is None:
                plane = lambda a, e: (wire_a[base + a : base + e, :] + 0.75) * ok
            else:
                plane = lambda a, e, n=n: buoy[n, a:e, :]
            if y0 > 0:
                above = plane(y0 - 1, y0 + BLOCK - 1)
            else:
                above = jnp.where(row > 0, pltpu.roll(c, 1, 0), 0.0)
            if y0 + BLOCK < ny:
                below = plane(y0 + 1, y0 + BLOCK + 1)
            else:
                below = jnp.where(row < ny - 1, pltpu.roll(c, BLOCK - 1, 0), 0.0)
            before = jnp.where(left, pltpu.roll(c, 1, 1), 0.0)
            after = jnp.where(right, pltpu.roll(c, nz - 1, 1), 0.0)
            faces = [
                0.5 * (b[j + 1] + c),
                0.5 * (b[j + 3] + c),
                0.5 * (above + c),
                0.5 * (below + c),
                0.5 * (before + c),
                0.5 * (after + c),
            ]
            total = sum(faces[1:], faces[0])
            co[j + 1, 0, ys, :] = 2.0 - mod * total
            faces[2] = jnp.where(row > 0, faces[2], 0.0)
            faces[3] = jnp.where(row < ny - 1, faces[3], 0.0)
            faces[4] = jnp.where(left, faces[4], 0.0)
            faces[5] = jnp.where(right, faces[5], 0.0)
            for i in range(6):
                co[j + 1, 1 + i, ys, :] = mod * faces[i]
            cs[j + 1, ys, :] = mod
            for s in range(both):
                ref = adj if s < shots else adj_in
                t = s % shots
                hot = hots[s : s + 1, :]
                if j >= 0:
                    k = (s * steps) * layers + j
                    p_out[s, j + 1, ys, :] = (
                        mod * spot(cols[ys, k : k + 1], hot) - ref[t, 0, n, ys, :]
                    )
                if 0 <= j < own:
                    k = (s * steps + 1) * layers + j
                    q_out[s, j, ys, :] = (
                        mod * spot(cols[ys, k : k + 1], hot) - ref[t, 1, n, ys, :]
                    )


def advance(co, j, fields, centre, extra, y0, ny, nz, total):
    ys = (y0, y0 + BLOCK)
    c = [co[j + 1, i, y0 : y0 + BLOCK, :] for i in range(7)]
    for s in range(total):
        u = fields(s, j, *ys)
        v = c[0] * u + extra(s, j)
        v = v + c[1] * fields(s, j - 1, *ys)
        v = v + c[2] * fields(s, j + 1, *ys)
        up = fields(s, j, y0 - 1, y0 + BLOCK - 1) if y0 > 0 else pltpu.roll(u, 1, 0)
        v = v + c[3] * up
        if y0 + BLOCK < ny:
            down = fields(s, j, y0 + 1, y0 + BLOCK + 1)
        else:
            down = pltpu.roll(u, BLOCK - 1, 0)
        v = v + c[4] * down
        v = v + c[5] * pltpu.roll(u, 1, 1)
        v = v + c[6] * pltpu.roll(u, nz - 1, 1)
        centre(s, j, v)


def chunk_body(first, shots, *refs):
    if first:
        co, cur, inner, p_in, q_in, wire_a, wire_b, mid, new = refs
    else:
        co, cur, inner, p_in, q_in, outer, mid, new = refs
    both, own, ny, nz = cur.shape

    def far(s, d, a, e):
        if not first:
            return outer[(s + shots) % both, d, a:e, :]
        ref = wire_b if s < shots else wire_a
        base = ((s % shots) * own + d) * ny
        return ref[base + a : base + e, :]

    def fields(s, j, a, e):
        if j < 0:
            return far(s, -1 - j, a, e)
        if j < own:
            return cur[s, j, a:e, :]
        return inner[(s + shots) % both, 2 * own - 1 - j, a:e, :]

    for y0 in range(0, ny, BLOCK):
        ys = slice(y0, y0 + BLOCK)

        def extra(s, j):
            if first and j < 0:
                ref = wire_b if s < shots else wire_a
                base = (shots * own + s % shots) * ny
                return -ref[base + y0 : base + y0 + BLOCK, :]
            return p_in[s, j + 1, ys, :]

        def put(s, j, v):
            mid[s, j + 1, ys, :] = v

        for j in range(-1, own + 1):
            advance(co, j, fields, put, extra, y0, ny, nz, both)

    def middle(s, j, a, e):
        return mid[s, j + 1, a:e, :]

    for y0 in range(0, ny, BLOCK):
        ys = slice(y0, y0 + BLOCK)

        def put(s, j, v):
            new[s, j, ys, :] = v

        for j in range(own):
            advance(co, j, middle, put, lambda s, j: q_in[s, j, ys, :], y0, ny, nz, both)


def image_body(steps, step, first, last, *refs):
    refs = list(refs)
    mid, new, saved, saved_in = refs[:4]
    del refs[:4]
    if not first:
        img_in = refs.pop(0)
    if last:
        slow, img = refs
    else:
        cols, hots, cs, outer_cols, img, p_out, q_out = refs
    both, own, ny, nz = new.shape
    shots, _, layers, _, _ = saved.shape
    level = steps - step
    for y0 in range(0, ny, BLOCK):
        ys = slice(y0, y0 + BLOCK)
        for j in range(own):
            n = native(j, layers)
            acc = None if first else img_in[j, ys, :]
            for s in range(both):
                ref = saved if s < shots else saved_in
                t = s % shots
                f = [ref[t, level + 1 - i, n, ys, :].astype(F32) for i in range(4)]
                term = mid[s, j + 1, ys, :] * (f[0] - 2.0 * f[1] + f[2])
                term = term + new[s, j, ys, :] * (f[1] - 2.0 * f[2] + f[3])
                acc = term if acc is None else acc + term
            if last:
                acc = acc / slow[n, ys, :]
            img[j, ys, :] = acc
        if last:
            continue
        for s in range(both):
            hot = hots[s : s + 1, :]
            for j in range(-1, own + 1):
                if j < 0:
                    k = s * (steps // 2) + (step + 2) // 2
                    col = outer_cols[ys, k : k + 1]
                else:
                    k = (s * steps + step + 2) * layers + j
                    col = cols[ys, k : k + 1]
                p_out[s, j + 1, ys, :] = cs[j + 1, ys, :] * spot(col, hot) - mid[s, j + 1, ys, :]
            for j in range(own):
                k = (s * steps + step + 3) * layers + j
                q_out[s, j, ys, :] = (
                    cs[j + 1, ys, :] * spot(cols[ys, k : k + 1], hot) - new[s, j, ys, :]
                )


def on_device(
    slowness,
    buoyancy,
    saved_fields,
    adj_states,
    residual_traces,
    receiver_depth,
    sample,
    noise_pred,
):
    gx_count = lax.axis_size("gx")
    gy_count = lax.axis_size("gy")
    pair_count = gy_count // 2
    gx_index = lax.axis_index("gx")
    gy_index = lax.axis_index("gy")
    lower = gy_index % 2 == 0
    pair = gy_index // 2
    shots, _, layers, ny, nz = adj_states.shape
    own = layers // 2
    both = 2 * shots
    steps = residual_traces.shape[1]
    has_outer = jnp.where(lower, gx_index > 0, gx_index < gx_count - 1)

    outer_perm = []
    across_perm = []
    for z in range(gx_count - 1):
        for p in range(pair_count):
            a = z * gy_count + 2 * p
            b = (z + 1) * gy_count + 2 * p
            outer_perm += [(a + 1, b), (b, a + 1)]
            across_perm += [(a, b), (b + 1, a + 1)]
    inner_perm = [(g, g ^ 1) for g in range(gy_count)]

    def to_outer(v):
        return lax.ppermute(v, ("gx", "gy"), outer_perm)

    def to_inner(v):
        return lax.ppermute(v, "gy", inner_perm)

    def orient(v, dim):
        return jnp.where(lower, v, jnp.flip(v, dim))

    scale0 = wire_scale(6.0 + time_square * 2.0 * 6.0)
    bounds = field_bounds(steps)

    adj_in = to_inner(adj_states)
    traces = orient(residual_traces, 2).astype(F32)
    lanes = lax.broadcasted_iota(jnp.int32, (shots, nz), 1)
    hot = (lanes == receiver_depth[:, None]).astype(F32)
    notes = jnp.concatenate([jnp.flip(traces, 2).reshape(-1, ny), hot], axis=0)
    notes_in = to_inner(notes)

    def columns(t):
        flat = t.reshape(-1, ny)
        return jnp.pad(flat, ((0, -flat.shape[0] % 128), (0, 0))).T

    rim_steps = list(range(0, steps, 2))

    def rim_rows(j):
        r = jnp.stack([traces[:, k, j] for k in rim_steps], 1).reshape(-1, ny)
        return jnp.pad(r, ((0, 16 - r.shape[0]), (0, 0)))

    rows = jnp.concatenate([rim_rows(0), rim_rows(layers - 1)], axis=0)
    size_a = (shots * own + shots + own + 1) * ny + 16
    size_b = (shots * own + shots) * ny + 16
    payload_a, payload_b = call(
        functools.partial(payload_body, steps, scale0),
        [(size_a, nz), (size_b, nz)],
        adj_states,
        buoyancy,
        slowness,
        columns(traces),
        hot,
        rows,
        name="payload",
    )
    got_a = to_outer(payload_a.astype(WIRE))
    got_b = lax.ppermute(payload_b.astype(WIRE), ("gx", "gy"), across_perm)
    saved_in = to_inner(saved_fields)
    wire_a = got_a.astype(F32) * (1.0 / scale0)
    wire_b = got_b.astype(F32) * (1.0 / scale0)

    n_tr = shots * steps * layers
    traces_in = notes_in[:n_tr].reshape(shots, steps, layers, ny)
    hots = jnp.concatenate([hot, notes_in[n_tr:]], axis=0)
    cols = columns(jnp.concatenate([traces, traces_in], axis=0))
    valid = jnp.broadcast_to(has_outer.astype(F32), (8, nz))
    half = (both, own, ny, nz)
    rim = (both, own + 2, ny, nz)
    cur, inner, co, cs, p_term, q_term = call(
        functools.partial(prepare_body, steps),
        [half, half, (own + 2, 7, ny, nz), (own + 2, ny, nz), rim, half],
        adj_states,
        adj_in,
        buoyancy,
        slowness,
        wire_a,
        cols,
        hots,
        valid,
        name="prepare",
    )
    n_rim = shots * len(rim_steps)
    outer_cols = columns(
        jnp.concatenate([wire_b[-16:][:n_rim], wire_a[-16:][:n_rim]], axis=0)
    )
    img = None
    for step in range(0, steps, 2):
        first = step == 0
        last = step + 2 >= steps
        if first:
            far = [wire_a, wire_b]
        else:
            scale = wire_scale(bounds[step])
            far = [to_outer((cur * scale).astype(WIRE)).astype(F32) * (1.0 / scale)]
            inner = to_inner(cur)
        if not first:
            tail = [] if img is None else [img]
            img, p_term, q_term = call(
                functools.partial(image_body, steps, step - 2, img is None, False),
                [(own, ny, nz), rim, half],
                mid,
                cur,
                saved_fields,
                saved_in,
                *tail,
                cols,
                hots,
                cs,
                outer_cols,
                name="image",
            )
        mid, cur = call(
            functools.partial(chunk_body, first, shots),
            [rim, half],
            co,
            cur,
            inner,
            p_term,
            q_term,
            *far,
            name="chunk",
        )
    back = to_inner(cur[shots:])
    shots_total = shots * gy_count
    (grad,) = call(
        functools.partial(image_body, steps, steps - 2, steps == 2, True),
        [(own, ny, nz)],
        mid,
        cur,
        saved_fields,
        saved_in,
        *([] if img is None else [img]),
        slowness,
        name="image",
    )
    grad = grad * (2.0 / (steps * shots_total))

    pair_rows = ny // pair_count
    padded = jnp.pad(grad, ((0, 0), (1, 1), (0, 0)))
    slices = [padded[:, q * pair_rows : (q + 1) * pair_rows + 2] for q in range(pair_count)]

    def slice_of(q):
        out = slices[0]
        for i in range(1, pair_count):
            out = jnp.where(q == i, slices[i], out)
        return out

    red = slice_of(pair)
    pieces = []
    for d in range(1, pair_count):
        perm = [
            (2 * p + e, 2 * ((p + d) % pair_count) + e)
            for p in range(pair_count)
            for e in range(2)
        ]
        pieces.append(lax.ppermute(slice_of((pair + d) % pair_count), "gy", perm))
    adj_last = orient(jnp.concatenate([cur[:shots], jnp.flip(back, 1)], axis=1), 1)
    pieces, adj_last = lax.optimization_barrier((pieces, adj_last))
    for piece in pieces:
        red = red + piece
    far = to_outer(red[:1, 1:-1])
    near = to_inner(red[own - 1 : own, 1:-1])
    centre = red[:, 1:-1]
    tall = jnp.concatenate([far, centre, near], axis=0)
    precond = 0.5 * centre + 0.125 * (tall[2:] + tall[:-2] + red[:, 2:] + red[:, :-2])
    part = pair_rows // 2
    keep = jnp.where(lower, precond[:, :part], precond[:, part:])
    give = jnp.where(lower, precond[:, part:], precond[:, :part])
    got = to_inner(give)
    precond_grad = orient(jnp.concatenate([keep, jnp.flip(got, 0)], axis=0), 0)
    sample_next = 1.02 * (sample - 0.2 * noise_pred.astype(F32)) - 0.5 * precond_grad
    return (adj_last, precond_grad, sample_next)


def solution(mesh):
    return jax.shard_map(
        on_device,
        mesh=mesh,
        in_specs=(
            P(("grp", "gx"), None, None),
            P(("grp", "gx"), None, None),
            P("gy", None, ("grp", "gx"), None, None),
            P("gy", None, ("grp", "gx"), None, None),
            P("gy", None, ("grp", "gx"), None),
            P(("grp", "gy")),
            P(("grp", "gx"), "gy", None),
            P(("grp", "gx"), "gy", None),
        ),
        out_specs=(
            P("gy", ("grp", "gx"), None, None),
            P(("grp", "gx"), "gy", None),
            P(("grp", "gx"), "gy", None),
        ),
        check_vma=False,
    )
```

time: 118 us -> 69.1 us (0.59)
  waiting for transfers between devices: 41.5 us -> 11.6 us
  starting transfers between devices: 44.2 us -> 21.3 us
  between operations: 14.6 us -> 1.28 us
  Pallas kernels: 0 us -> 12.1 us
  local copies, waits for them, and re-layouts: 5.4 us -> 14.3 us
  other arithmetic: 11.7 us -> 7.53 us
    reduce_scatter x1 -> x0, waiting for transfers between devices: 26.9 us -> none  [on_device(): lax.psum_scatter(grad_part, 'gy', scatter_dimension=1, tiled=True)]
    ppermute x16 -> x14, starting transfers between devices: 44.2 us -> 21.3 us  [the longest x4 15.4 us: to_outer(): return lax.ppermute(v, ('gx', 'gy'), outer_perm)]
    pallas_call x0 -> x8, Pallas kernels: none -> 12.1 us  [call(): pl.pallas_call(body, out_shape=tuple((jax.ShapeDtypeStruct(s, F32) for s...]
    unnamed x18 -> x44, local copies, waits for them, and re-layouts: 2.96 us -> 11.6 us
    convert_element_type x3 -> x6, other arithmetic: 0.09 us -> 3.73 us  [the longest x2 1.53 us: on_device(): far = [to_outer((cur * scale).astype(WIRE)).astype(F32) * (1.0 / scale)]]
    ppermute x16 -> x14, waiting for transfers between devices: 14.6 us -> 11.6 us  [the longest x1 5.17 us: on_device(): got_b = lax.ppermute(payload_b.astype(WIRE), ('gx', 'gy'), across_perm)]
    add x5 -> x2, other arithmetic: 2.62 us -> 0.05 us  [the longest x1 0.03 us: on_device(): 0.5 * centre + 0.125 * (tall[2:] + tall[:-2] + red[:, 2:] + red[:, :-2])]
    mul x26 -> x5, other arithmetic: 4.38 us -> 2.12 us  [the longest x2 1.05 us: on_device(): far = [to_outer((cur * scale).astype(WIRE)).astype(F32) * (1.0 / scale)]]
  transfers between devices with their start and end apart: 17 -> 14, of which waited for: 9 -> 5; matrix products, arithmetic and copies ran while one was open for 2% -> 12% of each run, Pallas kernels for 0% -> 13%
where the time goes in v2:
time: 69.1 us; the launch traced here: 68.2 us
  starting transfers between devices  21.3 us (31%)
  local copies, waits for them, and re-layouts  14.3 us (21%)
  Pallas kernels  12.1 us (18%)
  waiting for transfers between devices  11.6 us (17%)
  other arithmetic  7.53 us (11%)
  between operations  1.28 us (2%)
    ppermute x4, starting transfers between devices, to_outer(): return lax.ppermute(v, ('gx', 'gy'), outer_perm)  15.4 us
    pallas_call x8, Pallas kernels, call(): pl.pallas_call(body, out_shape=tuple((jax.ShapeDtypeStruct(s, F32) for s...  12.1 us
    unnamed x44, local copies, waits for them, and re-layouts  11.6 us
    ppermute x1, waiting for transfers between devices, on_device(): got_b = lax.ppermute(payload_b.astype(WIRE), ('gx', 'gy'), across_perm)  5.17 us
    ppermute x4, waiting for transfers between devices, to_outer(): return lax.ppermute(v, ('gx', 'gy'), outer_perm)  4.42 us
    ppermute x8, starting transfers between devices, to_inner(): return lax.ppermute(v, 'gy', inner_perm)  3.06 us
    ppermute x1, starting transfers between devices, on_device(): pieces.append(lax.ppermute(slice_of((pair + d) % pair_count), 'gy', perm))  1.61 us
    convert_element_type x2, other arithmetic, on_device(): far = [to_outer((cur * scale).astype(WIRE)).astype(F32) * (1.0 / scale)]  1.53 us
  transfers between devices with their start and end apart: 14, of which 5 were waited for; matrix products, arithmetic and copies ran while one was open for 12% of the time, Pallas kernels for 13%

profile of v2, /device:TPU:1, one launch (start us, length us, event | category | flops | bytes accessed | tf_op | source)
XLA Modules:
  0.0 68.2 jit_solution(1012846687175565843)
XLA Ops:
  0.6 0.7 %rev.24 = bf16[2,6,4,128]{3,2,1,0:T(4,128)(2,1)S(1)} reverse(bf16[2,6,4,128]{3,2,1,0:T(4,128)(2,1)} %param.12), dimensions={2} | reverse | bytes 24576 | tf_op jit(solution)/shard_map/jit(_flip)/rev | solution.py:318
  1.4 0.7 %compare_convert_fusion.hots = f32[2,128]{1,0:T(2,128)S(1)} fusion(s32[2]{0:T(128)} %param.13), kind=kLoop, calls=%fused_computation.38 | loop fusion | flops 512 | bytes 1032 | tf_op jit(solution)/shard_map/convert_element_type | solution.py:326
  2.2 0.8 %collective-permute-start.2 = (f32[50,128]{1,0:T(8,128)S(1)}, f32[50,128]{1,0:T(8,128)S(1)}, u32[]{:S(2)}, u32[]{:S(2)}) collective-permute-start(f32[50,128]{1,0:T(8,128)S(1)} %pad_maximum_fusion.5), channel_id=1, source_target_pairs={{0,1},{1,0},{2,3},{3,2},{4,5},{5,4},{6,7},{7,6},{8,9},{9,8},{10,11... | collective-permute-start | bytes 76808 | tf_op jit(solution)/shard_map/ppermute | solution.py:315
  3.0 0.1 collective-permute-start
  3.1 0.4 collective-permute-start.5
  3.6 0.1 copy.37
  3.7 0.0 copy-start.4
  3.7 1.2 %copy-done.4 = f32[2,2,4,128,128]{4,3,2,1,0:T(8,128)S(1)} copy-done((f32[2,2,4,128,128]{4,3,2,1,0:T(8,128)S(1)}, f32[2,2,4,128,128]{4,3,2,1,0:T(8,128)}, u32[]{:S(2)}) %copy-start.4) | copy-done | bytes 1048600
  4.9 0.9 %copy-done.6 = f32[4,128,128]{2,1,0:T(8,128)S(1)} copy-done((f32[4,128,128]{2,1,0:T(8,128)S(1)}, f32[4,128,128]{2,1,0:T(8,128)}, u32[]{:S(2)}) %copy-start.6) | copy-done | bytes 262168
  5.9 0.9 %copy-done.10 = f32[4,128,128]{2,1,0:T(8,128)S(1)} copy-done((f32[4,128,128]{2,1,0:T(8,128)S(1)}, f32[4,128,128]{2,1,0:T(8,128)}, u32[]{:S(2)}) %copy-start.10) | copy-done | bytes 262168
  6.8 0.2 payload.1
  7.0 0.0 copy-start.5
  7.0 0.0 copy-start.7
  7.0 0.0 copy-start.11
  7.0 0.8 %convert_element_type.49 = f16[1168,128]{1,0:T(8,128)(2,1)} convert(f32[1168,128]{1,0:T(8,128)S(1)} %get-tuple-element.25) | non-fusion elementwise | flops 149504 | bytes 897024 | tf_op jit(solution)/shard_map/convert_element_type | solution.py:354
  7.8 4.6 %collective-permute-start.1 = (f16[1168,128]{1,0:T(8,128)(2,1)}, f16[1168,128]{1,0:T(8,128)(2,1)}, u32[]{:S(2)}, u32[]{:S(2)}) collective-permute-start(f16[1168,128]{1,0:T(8,128)(2,1)} %convert_element_type.49), channel_id=1, source_target_pairs={{1,4},{4,1},{3,6},{6,3},{5,8},{8,5},{7,10},{10,7},{9,12},{12,9},{1... | collective-permute-start | bytes 897032 | tf_op jit(solution)/shard_map/ppermute | solution.py:312
  12.4 0.7 %convert_element_type.52 = f16[784,128]{1,0:T(8,128)(2,1)} convert(f32[784,128]{1,0:T(8,128)S(1)} %get-tuple-element.31) | non-fusion elementwise | flops 100352 | bytes 602112 | tf_op jit(solution)/shard_map/convert_element_type | solution.py:355
  13.1 1.3 %collective-permute-start.3 = (f16[784,128]{1,0:T(8,128)(2,1)}, f16[784,128]{1,0:T(8,128)(2,1)S(1)}, u32[]{:S(2)}, u32[]{:S(2)}) collective-permute-start(f16[784,128]{1,0:T(8,128)(2,1)} %convert_element_type.52), channel_id=1, source_target_pairs={{0,4},{5,1},{2,6},{7,3},{4,8},{9,5},{6,10},{11,7},{8,12},{13,9},{1... | collective-permute-start | bytes 602120 | tf_op jit(solution)/shard_map/ppermute | solution.py:355
  14.5 0.1 copy.44
  14.6 5.2 %collective-permute-done.3 = f16[784,128]{1,0:T(8,128)(2,1)S(1)} collective-permute-done((f16[784,128]{1,0:T(8,128)(2,1)}, f16[784,128]{1,0:T(8,128)(2,1)S(1)}, u32[]{:S(2)}, u32[]{:S(2)}) %collective-permute-start.3) | collective-permute-done | bytes 200736 | tf_op jit(solution)/shard_map/ppermute | solution.py:355
  19.8 1.0 %convert_multiply_fusion.wire_a.refs_5_ = f32[1168,128]{1,0:T(8,128)S(1)} fusion(f16[1168,128]{1,0:T(8,128)(2,1)} %collective-permute-done.1), kind=kLoop, calls=%fused_computation.1 | loop fusion | flops 299008 | bytes 897024 | tf_op jit(solution)/shard_map/mul | solution.py:357
  20.8 0.0 collective-permute-done.adj_in
  20.9 0.8 %prepare.1 = (f32[4,2,128,128]{3,2,1,0:T(8,128)S(1)}, f32[4,2,128,128]{3,2,1,0:T(8,128)S(1)}, f32[4,7,128,128]{3,2,1,0:T(8,128)S(1)}, f32[4,128,128]{2,1,0:T(8,1...) custom-call(f32[2,2,4,128,128]{4,3,2,1,0:T(8,128)S(1)} %copy-done.5, ...), custom_call_target="tpu_custom_call" | custom-call | flops 1000000 | bytes 4194304 | tf_op jit(solution)/shard_map/prepare/pallas_call | solution.py:33
  21.7 0.0 copy-start
  21.7 0.9 %chunk.3 = (f32[4,4,128,128]{3,2,1,0:T(8,128)S(1)}, f32[4,2,128,128]{3,2,1,0:T(8,128)S(1)}) custom-call(f32[4,7,128,128]{3,2,1,0:T(8,128)S(1)} %get-tuple-element.26.refs_0_, f32[4,2,128,128]{3,2,1,0:T(8,128)S(1)} %get-tuple-element.27.refs_1_, f32[4,2,128,128]{3,2,1,0:T(8,128)S(1)} %get-tuple-element.28.refs_2_, ...), custom_call_target="tpu_custom_call" | custom-call | flops 1000000 | bytes 4194304 | tf_op jit(solution)/shard_map/chunk/pallas_call | solution.py:33
  22.7 0.3 copy-done.1
  22.9 1.0 %copy-done.14 = f32[4,4,128,128]{3,2,1,0:T(8,128)} copy-done((f32[4,4,128,128]{3,2,1,0:T(8,128)}, f32[4,4,128,128]{3,2,1,0:T(8,128)S(1)}, u32[]{:S(2)}) %copy-start.14) | copy-done | bytes 1048600
  24.0 0.0 collective-permute-start.4
  24.0 0.8 %multiply_convert_fusion.1 = f16[4,2,128,128]{3,2,1,0:T(8,128)(2,1)} fusion(f32[4,2,128,128]{3,2,1,0:T(8,128)S(1)} %get-tuple-element.32.refs_1_), kind=kLoop, calls=%fused_computation.6 | loop fusion | flops 262144 | bytes 786432 | tf_op jit(solution)/shard_map/convert_element_type | solution.py:392
  24.7 3.6 %collective-permute-start.6 = (f16[4,2,128,128]{3,2,1,0:T(8,128)(2,1)}, f16[4,2,128,128]{3,2,1,0:T(8,128)(2,1)S(1)}, u32[]{:S(2)}, u32[]{:S(2)}) collective-permute-start(f16[4,2,128,128]{3,2,1,0:T(8,128)(2,1)} %multiply_convert_fusion.1), channel_id=1, source_target_pairs={{1,4},{4,1},{3,6},{6,3},{5,8},{8,5},{7,10},{10,7},{9,12},{12,9},{1... | collective-permute-start | bytes 786440 | tf_op jit(solution)/shard_map/ppermute | solution.py:312
  28.3 0.7 %copy.45 = f32[12,128]{0,1:T(8,128)} copy(f32[12,128]{1,0:T(8,128)S(1)} %pad_maximum_fusion.6) | data formatting | bytes 12288 | tf_op jit(solution)/shard_map/concatenate | solution.py:382
  29.1 0.8 %pad_bitcast_fusion.refs_7_.refs_8_ = f32[128,128]{1,0:T(8,128)S(1)} fusion(f32[12,128]{0,1:T(8,128)} %copy.45), kind=kLoop, calls=%fused_computation.22 | loop fusion | bytes 71680 | tf_op jit(solution)/shard_map/transpose | solution.py:332
  29.9 2.7 %collective-permute-done.6 = f16[4,2,128,128]{3,2,1,0:T(8,128)(2,1)S(1)} collective-permute-done((f16[4,2,128,128]{3,2,1,0:T(8,128)(2,1)}, f16[4,2,128,128]{3,2,1,0:T(8,128)(2,1)S(1)}, u32[]{:S(2)}, u32[]{:S(2)}) %collective-permute-start.6) | collective-permute-done | bytes 262176 | tf_op jit(solution)/shard_map/ppermute | solution.py:312
  32.7 0.0 collective-permute-done.5.refs_3_
  32.7 1.2 %copy-done.15 = f32[4,4,128,128]{3,2,1,0:T(8,128)S(1)} copy-done((f32[4,4,128,128]{3,2,1,0:T(8,128)S(1)}, f32[4,4,128,128]{3,2,1,0:T(8,128)}, u32[]{:S(2)}) %copy-start.15) | copy-done | bytes 1048600
  33.9 2.6 %image.3 = (f32[2,128,128]{2,1,0:T(8,128)S(1)}, f32[4,4,128,128]{3,2,1,0:T(8,128)S(1)}, f32[4,2,128,128]{3,2,1,0:T(8,128)S(1)}) custom-call(f32[4,4,128,128]{3,2,1,0:T(8,128)S(1)} %copy-done.15, f32[4,2,128,128]{3,2,1,0:T(8,128)S(1)} %get-tuple-element.32.refs_1_, bf16[2,8,4,128,128]{4,3,2,1,0:T(8,128)(2,1)S(1)} %copy-done, ...), custom_call_target="tpu_custom_call" | custom-call | flops 1000000 | bytes 4194304 | tf_op jit(solution)/shard_map/image/pallas_call | solution.py:33
  36.6 2.1 %chunk.4 = (f32[4,4,128,128]{3,2,1,0:T(8,128)S(1)}, f32[4,2,128,128]{3,2,1,0:T(8,128)S(1)}) custom-call(f32[4,7,128,128]{3,2,1,0:T(8,128)S(1)} %copy-done.2, f32[4,2,128,128]{3,2,1,0:T(8,128)S(1)} %get-tuple-element.32.refs_1_, f32[4,2,128,128]{3,2,1,0:T(8,128)} %collective-permute-done.4.refs_2_, f32[4,4,128,128]{3,2,1,0:T(8,128)S(1)} %get-tuple-element.35.refs_3_, ...), custom_call_target="tpu_custom_call" | custom-call | flops 1000000 | bytes 4194304 | tf_op jit(solution)/shard_map/chunk/pallas_call | solution.py:33
  38.7 1.0 %copy-done.12 = f32[4,4,128,128]{3,2,1,0:T(8,128)} copy-done((f32[4,4,128,128]{3,2,1,0:T(8,128)}, f32[4,4,128,128]{3,2,1,0:T(8,128)S(1)}, u32[]{:S(2)}) %copy-start.12) | copy-done | bytes 1048600
  39.7 0.0 collective-permute-start.7
  39.7 0.8 %multiply_convert_fusion = f16[4,2,128,128]{3,2,1,0:T(8,128)(2,1)} fusion(f32[4,2,128,128]{3,2,1,0:T(8,128)S(1)} %get-tuple-element.37.refs_1_), kind=kLoop, calls=%fused_computation.4 | loop fusion | flops 262144 | bytes 786432 | tf_op jit(solution)/shard_map/convert_element_type | solution.py:392
  40.5 3.7 %collective-permute-start.8 = (f16[4,2,128,128]{3,2,1,0:T(8,128)(2,1)}, f16[4,2,128,128]{3,2,1,0:T(8,128)(2,1)}, u32[]{:S(2)}, u32[]{:S(2)}) collective-permute-start(f16[4,2,128,128]{3,2,1,0:T(8,128)(2,1)} %multiply_convert_fusion), channel_id=1, source_target_pairs={{1,4},{4,1},{3,6},{6,3},{5,8},{8,5},{7,10},{10,7},{9,12},{12,9},{1... | collective-permute-start | bytes 786440 | tf_op jit(solution)/shard_map/ppermute | solution.py:312
  44.3 0.9 %copy-done.9 = f32[4,128,128]{2,1,0:T(8,128)S(1)} copy-done((f32[4,128,128]{2,1,0:T(8,128)S(1)}, f32[4,128,128]{2,1,0:T(8,128)}, u32[]{:S(2)}) %copy-start.9) | copy-done | bytes 262168
  45.2 1.2 %copy-done.13 = f32[4,4,128,128]{3,2,1,0:T(8,128)S(1)} copy-done((f32[4,4,128,128]{3,2,1,0:T(8,128)S(1)}, f32[4,4,128,128]{3,2,1,0:T(8,128)}, u32[]{:S(2)}) %copy-start.13) | copy-done | bytes 1048600
  46.4 0.9 %copy-done.19 = f32[2,128,128]{2,1,0:T(8,128)S(1)} copy-done((f32[2,128,128]{2,1,0:T(8,128)S(1)}, f32[2,128,128]{2,1,0:T(8,128)}, u32[]{:S(2)}) %copy-start.19) | copy-done | bytes 131096
  47.3 2.7 %image.4 = (f32[2,128,128]{2,1,0:T(8,128)S(1)}, f32[4,4,128,128]{3,2,1,0:T(8,128)S(1)}, f32[4,2,128,128]{3,2,1,0:T(8,128)S(1)}) custom-call(f32[4,4,128,128]{3,2,1,0:T(8,128)S(1)} %copy-done.13, f32[4,2,128,128]{3,2,1,0:T(8,128)S(1)} %get-tuple-element.37.refs_1_, bf16[2,8,4,128,128]{4,3,2,1,0:T(8,128)(2,1)S(1)} %copy-done, ...), custom_call_target="tpu_custom_call" | custom-call | flops 1000000 | bytes 4194304 | tf_op jit(solution)/shard_map/image/pallas_call | solution.py:33
  50.0 0.0 collective-permute-done.8
  50.0 1.0 %convert_multiply_fusion.1.refs_5_ = f32[4,2,128,128]{3,2,1,0:T(8,128)S(1)} fusion(f16[4,2,128,128]{3,2,1,0:T(8,128)(2,1)} %collective-permute-done.8), kind=kLoop, calls=%fused_computation.3 | loop fusion | flops 262144 | bytes 786432 | tf_op jit(solution)/shard_map/mul | solution.py:392
  51.0 0.0 copy-start.16
  51.0 0.8 %copy-done.16 = f32[4,2,128,128]{3,2,1,0:T(8,128)} copy-done((f32[4,2,128,128]{3,2,1,0:T(8,128)}, f32[4,2,128,128]{3,2,1,0:T(8,128)S(1)}, u32[]{:S(2)}) %copy-start.16) | copy-done | bytes 524312
  51.8 1.0 %copy-done.17 = f32[4,2,128,128]{3,2,1,0:T(8,128)S(1)} copy-done((f32[4,2,128,128]{3,2,1,0:T(8,128)S(1)}, f32[4,2,128,128]{3,2,1,0:T(8,128)}, u32[]{:S(2)}) %copy-start.17) | copy-done | bytes 524312
  52.9 1.0 %chunk.5 = (f32[4,4,128,128]{3,2,1,0:T(8,128)S(1)}, f32[4,2,128,128]{3,2,1,0:T(8,128)S(1)}) custom-call(f32[4,7,128,128]{3,2,1,0:T(8,128)S(1)} %copy-done.3, f32[4,2,128,128]{3,2,1,0:T(8,128)S(1)} %get-tuple-element.37.refs_1_, f32[4,2,128,128]{3,2,1,0:T(8,128)S(1)} %copy-done.17, f32[4,4,128,128]{3,2,1,0:T(8,128)S(1)} %get-tuple-element.40.refs_3_, ...), custom_call_target="tpu_custom_call" | custom-call | flops 1000000 | bytes 4194304 | tf_op jit(solution)/shard_map/chunk/pallas_call | solution.py:33
  53.9 0.1 collective-permute-start.10
  54.0 1.9 %image.5 = f32[2,128,128]{2,1,0:T(8,128)S(1)} custom-call(f32[4,4,128,128]{3,2,1,0:T(8,128)S(1)} %get-tuple-element.42.refs_0_, f32[4,2,128,128]{3,2,1,0:T(8,128)S(1)} %get-tuple-element.43.refs_1_, bf16[2,8,4,128,128]{4,3,2,1,0:T(8,128)(2,1)S(1)} %copy-done, bf16[2,8,4,128,128]{4,3,2,1,0:T(8,128)(2,1)} %collective-permute-done.5.refs_3_, ...), custom_call_target="tpu_custom_call" | custom-call | flops 1000000 | bytes 4194304 | tf_op jit(solution)/shard_map/image/pallas_call | solution.py:33
  55.9 0.0 copy-start.20
  55.9 0.0 copy-start.21
  55.9 1.6 %collective-permute-start.9 = (f32[2,66,128]{2,1,0:T(8,128)S(1)}, f32[2,66,128]{2,1,0:T(8,128)S(1)}, u32[]{:S(2)}, u32[]{:S(2)}) collective-permute-start(f32[2,66,128]{2,1,0:T(8,128)S(1)} %fusion.3), channel_id=1, source_target_pairs={{0,2},{1,3},{2,0},{3,1},{4,6},{5,7},{6,4},{7,5},{8,10},{9,11},{10,... | collective-permute-start | bytes 202760 | tf_op jit(solution)/shard_map/ppermute | solution.py:454
  57.6 0.8 %reverse_select_fusion = f32[2,4,128,128]{3,2,1,0:T(8,128)} fusion(f32[2,4,128,128]{3,2,1,0:T(8,128)S(1)} %pad_maximum_fusion, pred[]{:T(512)S(6)} %eq.21), kind=kLoop, calls=%fused_computation | loop fusion | flops 131072 | bytes 1048577 | tf_op jit(solution)/shard_map/jit(_where)/select_n | solution.py:318
  58.5 0.8 %collective-permute-done.9 = f32[2,66,128]{2,1,0:T(8,128)S(1)} collective-permute-done((f32[2,66,128]{2,1,0:T(8,128)S(1)}, f32[2,66,128]{2,1,0:T(8,128)S(1)}, u32[]{:S(2)}, u32[]{:S(2)}) %collective-permute-start.9) | collective-permute-done | bytes 67616 | tf_op jit(solution)/shard_map/ppermute | solution.py:454
  59.3 1.6 %collective-permute-start.11 = (f32[1,64,128]{2,1,0:T(8,128)S(1)}, f32[1,64,128]{2,1,0:T(8,128)S(1)}, u32[]{:S(2)}, u32[]{:S(2)}) collective-permute-start(f32[1,64,128]{2,1,0:T(8,128)S(1)} %get-tuple-element.51), channel_id=1, source_target_pairs={{0,1},{1,0},{2,3},{3,2},{4,5},{5,4},{6,7},{7,6},{8,9},{9,8},{10,11... | collective-permute-start | bytes 98312 | tf_op jit(solution)/shard_map/ppermute | solution.py:315
  61.0 3.4 %collective-permute-start.12 = (f32[1,64,128]{2,1,0:T(8,128)S(1)}, f32[1,64,128]{2,1,0:T(8,128)S(1)}, u32[]{:S(2)}, u32[]{:S(2)}) collective-permute-start(f32[1,64,128]{2,1,0:T(8,128)S(1)} %get-tuple-element.52), channel_id=1, source_target_pairs={{1,4},{4,1},{3,6},{6,3},{5,8},{8,5},{7,10},{10,7},{9,12},{12,9},{1... | collective-permute-start | bytes 98312 | tf_op jit(solution)/shard_map/ppermute | solution.py:312
  64.4 1.7 %collective-permute-done.12 = f32[1,64,128]{2,1,0:T(8,128)S(1)} collective-permute-done((f32[1,64,128]{2,1,0:T(8,128)S(1)}, f32[1,64,128]{2,1,0:T(8,128)S(1)}, u32[]{:S(2)}, u32[]{:S(2)}) %collective-permute-start.12) | collective-permute-done | bytes 32800 | tf_op jit(solution)/shard_map/ppermute | solution.py:312
  66.2 0.1 collective-permute-start.13
  66.3 1.2 %collective-permute-done.13 = f32[2,32,128]{2,1,0:T(8,128)S(1)} collective-permute-done((f32[2,32,128]{2,1,0:T(8,128)S(1)}, f32[2,32,128]{2,1,0:T(8,128)S(1)}, u32[]{:S(2)}, u32[]{:S(2)}) %collective-permute-start.13) | collective-permute-done | bytes 32800 | tf_op jit(solution)/shard_map/ppermute | solution.py:315
  67.5 0.7 multiply_subtract_fusion
  (65 shorter events, 0.5 us)
Async XLA Ops:
  2.2 12.2 %collective-permute-start.2 = (f32[50,128]{1,0:T(8,128)S(1)}, f32[50,128]{1,0:T(8,128)S(1)}, u32[]{:S(2)}, u32[]{:S(2)}) collective-permute-start(f32[50,128]{1,0:T(8,128)S(1)} %pad_maximum_fusion.5), channel_id=1, source_target_pairs={{0,1},{1,0},{2,3},{3,2},{4,5},{5,4},{6,7},{7,6},{8,9},{9,8},{10,11... | collective-permute-start | bytes 76808 | tf_op jit(solution)/shard_map/ppermute | solution.py:315
  3.0 17.9 %collective-permute-start = (f32[2,2,4,128,128]{4,3,2,1,0:T(8,128)}, f32[2,2,4,128,128]{4,3,2,1,0:T(8,128)S(1)}, u32[]{:S(2)}, u32[]{:S(2)}) collective-permute-start(f32[2,2,4,128,128]{4,3,2,1,0:T(8,128)} %adj.3), channel_id=1, source_target_pairs={{0,1},{1,0},{2,3},{3,2},{4,5},{5,4},{6,7},{7,6},{8,9},{9,8},{10,11... | collective-permute-start | bytes 3145736 | tf_op jit(solution)/shard_map/ppermute | solution.py:315
  3.1 29.6 %collective-permute-start.5 = (bf16[2,8,4,128,128]{4,3,2,1,0:T(8,128)(2,1)}, bf16[2,8,4,128,128]{4,3,2,1,0:T(8,128)(2,1)}, u32[]{:S(2)}, u32[]{:S(2)}) collective-permute-start(bf16[2,8,4,128,128]{4,3,2,1,0:T(8,128)(2,1)} %refs_2_.5), channel_id=1, source_target_pairs={{0,1},{1,0},{2,3},{3,2},{4,5},{5,4},{6,7},{7,6},{8,9},{9,8},{10,11... | collective-permute-start | bytes 6291464 | tf_op jit(solution)/shard_map/ppermute | solution.py:315
  3.7 1.2 %copy-start.4 = (f32[2,2,4,128,128]{4,3,2,1,0:T(8,128)S(1)}, f32[2,2,4,128,128]{4,3,2,1,0:T(8,128)}, u32[]{:S(2)}) copy-start(f32[2,2,4,128,128]{4,3,2,1,0:T(8,128)} %adj.3) | copy-start | bytes 3145732
  4.9 0.9 %copy-start.6 = (f32[4,128,128]{2,1,0:T(8,128)S(1)}, f32[4,128,128]{2,1,0:T(8,128)}, u32[]{:S(2)}) copy-start(f32[4,128,128]{2,1,0:T(8,128)} %refs_5_.1) | copy-start | bytes 786436
  5.9 0.9 %copy-start.10 = (f32[4,128,128]{2,1,0:T(8,128)S(1)}, f32[4,128,128]{2,1,0:T(8,128)}, u32[]{:S(2)}) copy-start(f32[4,128,128]{2,1,0:T(8,128)} %buoy.3) | copy-start | bytes 786436
  7.0 13.9 %copy-start.5 = (f32[2,2,4,128,128]{4,3,2,1,0:T(8,128)S(1)}, f32[2,2,4,128,128]{4,3,2,1,0:T(8,128)}, u32[]{:S(2)}) copy-start(f32[2,2,4,128,128]{4,3,2,1,0:T(8,128)} %adj.3) | copy-start | bytes 3145732
  7.0 13.9 %copy-start.7 = (f32[4,128,128]{2,1,0:T(8,128)S(1)}, f32[4,128,128]{2,1,0:T(8,128)}, u32[]{:S(2)}) copy-start(f32[4,128,128]{2,1,0:T(8,128)} %refs_5_.1) | copy-start | bytes 786436
  7.0 13.9 %copy-start.11 = (f32[4,128,128]{2,1,0:T(8,128)S(1)}, f32[4,128,128]{2,1,0:T(8,128)}, u32[]{:S(2)}) copy-start(f32[4,128,128]{2,1,0:T(8,128)} %buoy.3) | copy-start | bytes 786436
  7.8 12.0 %collective-permute-start.1 = (f16[1168,128]{1,0:T(8,128)(2,1)}, f16[1168,128]{1,0:T(8,128)(2,1)}, u32[]{:S(2)}, u32[]{:S(2)}) collective-permute-start(f16[1168,128]{1,0:T(8,128)(2,1)} %convert_element_type.49), channel_id=1, source_target_pairs={{1,4},{4,1},{3,6},{6,3},{5,8},{8,5},{7,10},{10,7},{9,12},{12,9},{1... | collective-permute-start | bytes 897032 | tf_op jit(solution)/shard_map/ppermute | solution.py:312
  13.1 6.7 %collective-permute-start.3 = (f16[784,128]{1,0:T(8,128)(2,1)}, f16[784,128]{1,0:T(8,128)(2,1)S(1)}, u32[]{:S(2)}, u32[]{:S(2)}) collective-permute-start(f16[784,128]{1,0:T(8,128)(2,1)} %convert_element_type.52), channel_id=1, source_target_pairs={{0,4},{5,1},{2,6},{7,3},{4,8},{9,5},{6,10},{11,7},{8,12},{13,9},{1... | collective-permute-start | bytes 602120 | tf_op jit(solution)/shard_map/ppermute | solution.py:355
  21.7 1.2 %copy-start.1 = (f32[4,7,128,128]{3,2,1,0:T(8,128)}, f32[4,7,128,128]{3,2,1,0:T(8,128)S(1)}, u32[]{:S(2)}) copy-start(f32[4,7,128,128]{3,2,1,0:T(8,128)S(1)} %get-tuple-element.26.refs_0_) | copy-start | bytes 5505028
  21.7 11.0 %copy-start.8 = (f32[4,128,128]{2,1,0:T(8,128)}, f32[4,128,128]{2,1,0:T(8,128)S(1)}, u32[]{:S(2)}) copy-start(f32[4,128,128]{2,1,0:T(8,128)S(1)} %get-tuple-element.34.refs_6_.refs_7_) | copy-start | bytes 786436
  21.7 11.0 %copy-start = (bf16[2,8,4,128,128]{4,3,2,1,0:T(8,128)(2,1)S(1)}, bf16[2,8,4,128,128]{4,3,2,1,0:T(8,128)(2,1)}, u32[]{:S(2)}) copy-start(bf16[2,8,4,128,128]{4,3,2,1,0:T(8,128)(2,1)} %refs_2_.5) | copy-start | bytes 6291460
  22.9 1.0 %copy-start.14 = (f32[4,4,128,128]{3,2,1,0:T(8,128)}, f32[4,4,128,128]{3,2,1,0:T(8,128)S(1)}, u32[]{:S(2)}) copy-start(f32[4,4,128,128]{3,2,1,0:T(8,128)S(1)} %get-tuple-element.33.refs_0_) | copy-start | bytes 3145732
  24.0 12.6 %collective-permute-start.4 = (f32[4,2,128,128]{3,2,1,0:T(8,128)S(1)}, f32[4,2,128,128]{3,2,1,0:T(8,128)}, u32[]{:S(2)}, u32[]{:S(2)}) collective-permute-start(f32[4,2,128,128]{3,2,1,0:T(8,128)S(1)} %get-tuple-element.32.refs_1_), channel_id=1, source_target_pairs={{0,1},{1,0},{2,3},{3,2},{4,5},{5,4},{6,7},{7,6},{8,9},{9,8},{10,11... | collective-permute-start | bytes 1572872 | tf_op jit(solution)/shard_map/ppermute | solution.py:315
  24.7 7.9 %collective-permute-start.6 = (f16[4,2,128,128]{3,2,1,0:T(8,128)(2,1)}, f16[4,2,128,128]{3,2,1,0:T(8,128)(2,1)S(1)}, u32[]{:S(2)}, u32[]{:S(2)}) collective-permute-start(f16[4,2,128,128]{3,2,1,0:T(8,128)(2,1)} %multiply_convert_fusion.1), channel_id=1, source_target_pairs={{1,4},{4,1},{3,6},{6,3},{5,8},{8,5},{7,10},{10,7},{9,12},{12,9},{1... | collective-permute-start | bytes 786440 | tf_op jit(solution)/shard_map/ppermute | solution.py:312
  32.7 1.2 %copy-start.15 = (f32[4,4,128,128]{3,2,1,0:T(8,128)S(1)}, f32[4,4,128,128]{3,2,1,0:T(8,128)}, u32[]{:S(2)}) copy-start(f32[4,4,128,128]{3,2,1,0:T(8,128)} %copy-done.14) | copy-start | bytes 3145732
  33.9 2.7 %copy-start.2 = (f32[4,7,128,128]{3,2,1,0:T(8,128)S(1)}, f32[4,7,128,128]{3,2,1,0:T(8,128)}, u32[]{:S(2)}) copy-start(f32[4,7,128,128]{3,2,1,0:T(8,128)} %copy-done.1) | copy-start | bytes 5505028
  36.6 2.1 %copy-start.18 = (f32[2,128,128]{2,1,0:T(8,128)}, f32[2,128,128]{2,1,0:T(8,128)S(1)}, u32[]{:S(2)}) copy-start(f32[2,128,128]{2,1,0:T(8,128)S(1)} %get-tuple-element.39.refs_4_) | copy-start | bytes 393220
  38.7 1.0 %copy-start.12 = (f32[4,4,128,128]{3,2,1,0:T(8,128)}, f32[4,4,128,128]{3,2,1,0:T(8,128)S(1)}, u32[]{:S(2)}) copy-start(f32[4,4,128,128]{3,2,1,0:T(8,128)S(1)} %get-tuple-element.38.refs_0_) | copy-start | bytes 3145732
  39.7 11.3 %collective-permute-start.7 = (f32[4,2,128,128]{3,2,1,0:T(8,128)S(1)}, f32[4,2,128,128]{3,2,1,0:T(8,128)S(1)}, u32[]{:S(2)}, u32[]{:S(2)}) collective-permute-start(f32[4,2,128,128]{3,2,1,0:T(8,128)S(1)} %get-tuple-element.37.refs_1_), channel_id=1, source_target_pairs={{0,1},{1,0},{2,3},{3,2},{4,5},{5,4},{6,7},{7,6},{8,9},{9,8},{10,11... | collective-permute-start | bytes 1572872 | tf_op jit(solution)/shard_map/ppermute | solution.py:315
  40.5 9.5 %collective-permute-start.8 = (f16[4,2,128,128]{3,2,1,0:T(8,128)(2,1)}, f16[4,2,128,128]{3,2,1,0:T(8,128)(2,1)}, u32[]{:S(2)}, u32[]{:S(2)}) collective-permute-start(f16[4,2,128,128]{3,2,1,0:T(8,128)(2,1)} %multiply_convert_fusion), channel_id=1, source_target_pairs={{1,4},{4,1},{3,6},{6,3},{5,8},{8,5},{7,10},{10,7},{9,12},{12,9},{1... | collective-permute-start | bytes 786440 | tf_op jit(solution)/shard_map/ppermute | solution.py:312
  44.2 1.0 %copy-start.9 = (f32[4,128,128]{2,1,0:T(8,128)S(1)}, f32[4,128,128]{2,1,0:T(8,128)}, u32[]{:S(2)}) copy-start(f32[4,128,128]{2,1,0:T(8,128)} %copy-done.8) | copy-start | bytes 786436
  45.2 1.2 %copy-start.13 = (f32[4,4,128,128]{3,2,1,0:T(8,128)S(1)}, f32[4,4,128,128]{3,2,1,0:T(8,128)}, u32[]{:S(2)}) copy-start(f32[4,4,128,128]{3,2,1,0:T(8,128)} %copy-done.12) | copy-start | bytes 3145732
  46.4 0.9 %copy-start.19 = (f32[2,128,128]{2,1,0:T(8,128)S(1)}, f32[2,128,128]{2,1,0:T(8,128)}, u32[]{:S(2)}) copy-start(f32[2,128,128]{2,1,0:T(8,128)} %copy-done.18) | copy-start | bytes 393220
  47.3 4.5 %copy-start.3 = (f32[4,7,128,128]{3,2,1,0:T(8,128)S(1)}, f32[4,7,128,128]{3,2,1,0:T(8,128)}, u32[]{:S(2)}) copy-start(f32[4,7,128,128]{3,2,1,0:T(8,128)} %copy-done.1) | copy-start | bytes 5505028
  51.0 0.8 %copy-start.16 = (f32[4,2,128,128]{3,2,1,0:T(8,128)}, f32[4,2,128,128]{3,2,1,0:T(8,128)S(1)}, u32[]{:S(2)}) copy-start(f32[4,2,128,128]{3,2,1,0:T(8,128)S(1)} %collective-permute-done.7.refs_2_) | copy-start | bytes 1572868
  51.8 1.0 %copy-start.17 = (f32[4,2,128,128]{3,2,1,0:T(8,128)S(1)}, f32[4,2,128,128]{3,2,1,0:T(8,128)}, u32[]{:S(2)}) copy-start(f32[4,2,128,128]{3,2,1,0:T(8,128)} %copy-done.16) | copy-start | bytes 1572868
  53.9 3.6 %collective-permute-start.10 = (f32[2,2,128,128]{3,2,1,0:T(8,128)S(1)}, f32[2,2,128,128]{3,2,1,0:T(8,128)S(1)}, u32[]{:S(2)}, u32[]{:S(2)}) collective-permute-start(f32[2,2,128,128]{3,2,1,0:T(8,128)S(1)} %get-tuple-element.50), channel_id=1, source_target_pairs={{0,1},{1,0},{2,3},{3,2},{4,5},{5,4},{6,7},{7,6},{8,9},{9,8},{10,11... | collective-permute-start | bytes 786440 | tf_op jit(solution)/shard_map/ppermute | solution.py:315
  55.9 11.6 %copy-start.20 = (f32[4,32,128]{2,1,0:T(8,128)S(1)}, f32[4,32,128]{2,1,0:T(8,128)}, u32[]{:S(2)}) copy-start(f32[4,32,128]{2,1,0:T(8,128)} %param.14) | copy-start | bytes 196612
  55.9 11.6 %copy-start.21 = (bf16[4,32,128]{2,1,0:T(8,128)(2,1)S(1)}, bf16[4,32,128]{2,1,0:T(8,128)(2,1)}, u32[]{:S(2)}) copy-start(bf16[4,32,128]{2,1,0:T(8,128)(2,1)} %param.15) | copy-start | bytes 98308
  55.9 3.4 %collective-permute-start.9 = (f32[2,66,128]{2,1,0:T(8,128)S(1)}, f32[2,66,128]{2,1,0:T(8,128)S(1)}, u32[]{:S(2)}, u32[]{:S(2)}) collective-permute-start(f32[2,66,128]{2,1,0:T(8,128)S(1)} %fusion.3), channel_id=1, source_target_pairs={{0,2},{1,3},{2,0},{3,1},{4,6},{5,7},{6,4},{7,5},{8,10},{9,11},{10,... | collective-permute-start | bytes 202760 | tf_op jit(solution)/shard_map/ppermute | solution.py:454
  59.3 5.1 %collective-permute-start.11 = (f32[1,64,128]{2,1,0:T(8,128)S(1)}, f32[1,64,128]{2,1,0:T(8,128)S(1)}, u32[]{:S(2)}, u32[]{:S(2)}) collective-permute-start(f32[1,64,128]{2,1,0:T(8,128)S(1)} %get-tuple-element.51), channel_id=1, source_target_pairs={{0,1},{1,0},{2,3},{3,2},{4,5},{5,4},{6,7},{7,6},{8,9},{9,8},{10,11... | collective-permute-start | bytes 98312 | tf_op jit(solution)/shard_map/ppermute | solution.py:315
  61.0 5.2 %collective-permute-start.12 = (f32[1,64,128]{2,1,0:T(8,128)S(1)}, f32[1,64,128]{2,1,0:T(8,128)S(1)}, u32[]{:S(2)}, u32[]{:S(2)}) collective-permute-start(f32[1,64,128]{2,1,0:T(8,128)S(1)} %get-tuple-element.52), channel_id=1, source_target_pairs={{1,4},{4,1},{3,6},{6,3},{5,8},{8,5},{7,10},{10,7},{9,12},{12,9},{1... | collective-permute-start | bytes 98312 | tf_op jit(solution)/shard_map/ppermute | solution.py:312
  66.2 1.3 %collective-permute-start.13 = (f32[2,32,128]{2,1,0:T(8,128)S(1)}, f32[2,32,128]{2,1,0:T(8,128)S(1)}, u32[]{:S(2)}, u32[]{:S(2)}) collective-permute-start(f32[2,32,128]{2,1,0:T(8,128)S(1)} %get-tuple-element.54), channel_id=1, source_target_pairs={{0,1},{1,0},{2,3},{3,2},{4,5},{5,4},{6,7},{7,6},{8,9},{9,8},{10,11... | collective-permute-start | bytes 98312 | tf_op jit(solution)/shard_map/ppermute | solution.py:315
